TPU v7x, 256 devices: a whole 4x4x8 slice. The times are simulated.
256 devices in a mesh: dp: 32 (over x, z), expert: 8 (over y, core).
Axes of the slice: x: 4, y: 4, z: 8, core: 2. Of those that a mesh axis runs over, the one named last changes fastest.
Arguments:
- saved_inputs: bfloat16 [32, 8, 1024, 4096], P('dp', 'expert'), may hold values from -6 to 6
- saved_grads: bfloat16 [32, 8, 1024, 1536], P('dp', 'expert'), may hold values from -6 to 6
- row_counts: int32 [32, 8], P('dp', 'expert'), may hold values from 1 to 1024, as said below
- row_seq: int32 [32, 8, 1024], P('dp', 'expert'), may hold values from 0 to 255
- proj_in: bfloat16 [4096, 32], replicated, may hold values from -0.09375 to 0.09375
- proj_out: bfloat16 [1536, 32], replicated, may hold values from -0.15625 to 0.15625
Outputs:
- logged: bfloat16 [8, 8192, 1024], P(None, ('dp', 'expert'))
- fisher: float32 [1024, 8, 1024], P('dp', 'expert')
Inputs may be any that keep to these rules, and one draw needn't show every extreme that they name: Slots from row_counts on are padding with arbitrary contents; row_counts reaches 1024 for some expert in every draw.
All inputs are finite; a program needn't handle non-finite values.
Results may differ from a plain program's by a relative error of at most 0.012.
Values may be sent and summed in bfloat16 or wider, within the bound.
No kernel may reach another device: no remote copies, remote signals or barrier semaphores. Data moves between devices by JAX's collectives and lax.ppermute only.
A program may use at most 64 MiB of HBM per device.

v0:
```python
import functools

import jax
import jax.numpy as jnp
from jax import lax
from jax.sharding import Mesh
from jax.sharding import PartitionSpec as P

SEQ_DEV = 256
DP = ("dp_0", "dp_1")
DP_EXPERT = ("dp_0", "dp_1", "expert")


def over_axes(value, axes):
    return functools.reduce(lax.psum, axes, value)


def own_rows_2(terms, axes):
    total = terms.astype(jnp.bfloat16)
    for axis in axes:
        total = lax.psum_scatter(total, axis, scatter_dimension=0, tiled=True)
    return total.astype(jnp.float32)


def body(saved_inputs, saved_grads, row_counts, row_seq, proj_in, proj_out):
    inputs = saved_inputs[0]
    row_grads = saved_grads[0]
    counts = row_counts[0]
    seq_ids = row_seq[0]
    experts, capacity, width = inputs.shape
    proj_rank = proj_in.shape[1]
    square = proj_rank * proj_rank
    in_proj = jnp.dot(
        inputs.reshape(experts * capacity, width), proj_in, preferred_element_type=jnp.float32
    )
    out_proj = jnp.dot(
        row_grads.reshape(experts * capacity, row_grads.shape[2]),
        proj_out,
        preferred_element_type=jnp.float32,
    )
    outer_rows = (
        (out_proj[:, :, None] * in_proj[:, None, :])
        .reshape(experts, capacity, square)
        .astype(jnp.bfloat16)
    )
    slot_ids = jnp.arange(capacity, dtype=jnp.int32)
    is_live = slot_ids[None, :] < counts[:, None]
    member = (seq_ids[:, None, :] == jnp.arange(SEQ_DEV, dtype=jnp.int32)[None, :, None]) & is_live[
        :, None, :
    ]
    onehot = member.astype(jnp.bfloat16)
    seq_grads = jnp.einsum(
        "esc,eck->esk", onehot, outer_rows, preferred_element_type=jnp.float32
    ).astype(jnp.bfloat16)
    logged = lax.all_to_all(seq_grads, "expert", split_axis=1, concat_axis=0, tiled=True)
    totals = over_axes(counts.astype(jnp.float32), DP)
    fisher = own_rows_2(
        jnp.einsum("esi,esj->iej", seq_grads, seq_grads, preferred_element_type=jnp.float32), DP
    )
    return (logged, fisher / totals[None, :, None])


def solution(mesh):
    split = Mesh(mesh.devices.reshape(4, 8, mesh.shape["expert"]), ("dp_0", "dp_1", "expert"))
    in_specs = (
        P(DP, "expert", None, None),
        P(DP, "expert", None, None),
        P(DP, "expert"),
        P(DP, "expert", None),
        P(),
        P(),
    )
    out_specs = (P(None, DP_EXPERT, None), P(DP, "expert", None))
    return jax.shard_map(body, mesh=split, in_specs=in_specs, out_specs=out_specs, check_vma=False)
```

profile of v0, /device:TPU:2, one launch (start us, length us, event | category | flops | bytes accessed | tf_op | source)
XLA Modules:
  0.0 143.4 jit_solution(14997110314798607037)
XLA Ops:
  7.2 0.0 copy-start
  7.2 0.0 reduce-scatter.2.cloned.1.call-start
  8.0 0.0 copy-start.2
  8.0 6.1 %fusion = f32[1024,32]{0,1:T(8,128)S(1)} fusion(bf16[4096,32]{0,1:T(8,128)(2,1)} %param.10, bf16[1,1,1024,4096]{3,2,1,0:T(8,128)(2,1)} %param.6), kind=kOutput, calls=%fused_computation | convolution fusion | flops 268435456 | bytes 8781824 | tf_op jit(solution)/shard_map/dot_general | solution.py:33
  14.1 0.0 copy-done
  14.1 0.0 copy-done.2
  14.1 0.0 copy-start.3
  14.1 1.0 fusion.2
  15.1 0.6 multiply_convert_fusion
  15.7 0.8 convolution_convert_fusion
  16.5 0.0 copy-start.1
  16.5 0.8 copy-done.1
  17.3 2.1 %convert_bitcast_fusion = bf16[1024,1,1024]{0,2,1:T(8,128)(2,1)} fusion(bf16[256,1024]{1,0:T(8,128)(2,1)S(1)} %convolution_convert_fusion), kind=kOutput, calls=%fused_computation.5 | convolution fusion | flops 537919488 | bytes 2621440 | tf_op jit(solution)/shard_map/esi,esj->iej/dot_general | solution.py:58
  19.4 0.0 reduce-scatter.2.cloned.1.call-update
  19.4 0.0 all-reduce.3.cloned.1.call-start
  19.4 34.1 %reduce-scatter.2.cloned.1.call-done = bf16[256,1,1024]{0,2,1:T(8,128)(2,1)} async-done(((bf16[1024,1,1024]{0,2,1:T(8,128)(2,1)}), bf16[256,1,1024]{0,2,1:T(8,128)(2,1)}) %reduce-scatter.2.cloned.1.call-update) | async-done | bytes 524304 | tf_op jit(solution)/shard_map/reduce_scatter | solution.py:21
  53.5 3.6 %copy.15 = bf16[256,1,1024]{2,1,0:T(2,128)(2,1)} copy(bf16[256,1,1024]{0,2,1:T(8,128)(2,1)} %reduce-scatter.2.cloned.1.call-done) | data formatting | bytes 1048576 | tf_op jit(solution)/shard_map/reduce_scatter | solution.py:21
  57.1 0.0 all-reduce.3.cloned.1.call-update
  57.1 2.8 %copy.18 = bf16[1,256,1024]{2,0,1:T(2,128)(2,1)} copy(bf16[1,256,1024]{2,1,0:T(8,128)(2,1)} %bitcast.28) | data formatting | bytes 1048576 | tf_op jit(solution)/shard_map/convert_element_type | solution.py:54
  59.9 0.5 broadcast.31
  60.4 5.5 %reduce = bf16[256,1024]{1,0:T(8,128)(2,1)} reduce(bf16[256,1,1024]{2,1,0:T(2,128)(2,1)} %bitcast.30, bf16[]{:T(256)} %broadcast.31), dimensions={1}, to_apply=%bitcast.26.reduce_sub_computation | reduce | bytes 1048578
  65.9 2.2 %reshape.76 = bf16[8,2,16384]{2,1,0:T(2,128)(2,1)} reshape(bf16[256,1024]{1,0:T(8,128)(2,1)} %reduce) | data formatting | bytes 1048576
  68.1 4.3 %all-to-all-start = ((bf16[8,2,16384]{2,1,0:T(2,128)(2,1)}), bf16[8,2,16384]{2,1,0:T(2,128)(2,1)}, u32[]{:S(2)}, u32[]{:S(2)}) async-start(bf16[8,2,16384]{2,1,0:T(2,128)(2,1)} %reshape.76), calls=%async_computation | async-start | bytes 1048576 | tf_op jit(solution)/shard_map/all_to_all | solution.py:55
  72.4 10.6 %psum.14 = f32[1]{0:T(128)} all-reduce(f32[1]{0:T(128)} %bitcast.8), channel_id=1, replica_groups=mesh['dp_0'=4,'dp_1'=8,'expert'=8] {'dp_0'}, use_global_device_ids=true, to_apply=%region_2.0 | all-reduce | flops 1 | bytes 8 | tf_op jit(solution)/shard_map/psum | solution.py:15
  83.0 18.1 %psum.15 = f32[]{:T(128)} all-reduce(f32[]{:T(128)} %bitcast.9), channel_id=1, replica_groups=mesh['dp_0'=4,'dp_1'=8,'expert'=8] {'dp_1'}, use_global_device_ids=true, to_apply=%region_3.0 | all-reduce | flops 1 | bytes 8 | tf_op jit(solution)/shard_map/psum | solution.py:15
  101.1 0.0 copy-done.4
  101.1 0.6 dynamic-slice
  102.4 0.0 all-to-all-done
  102.4 3.5 %reshape.77 = bf16[256,1,1024]{2,1,0:T(2,128)(2,1)} reshape(bf16[8,2,16384]{2,1,0:T(2,128)(2,1)} %all-to-all-done) | data formatting | bytes 1048576
  105.9 2.2 %copy.16 = bf16[1,256,1024]{2,1,0:T(8,128)(2,1)} copy(bf16[1,256,1024]{2,0,1:T(2,128)(2,1)} %bitcast.29) | data formatting | bytes 1048576
  108.1 26.2 %all-reduce.3.cloned.1.call-done = bf16[256,1,1024]{2,1,0:T(2,128)(2,1)} async-done(((bf16[256,1,1024]{2,1,0:T(2,128)(2,1)}), bf16[256,1,1024]{2,1,0:T(2,128)(2,1)}) %all-reduce.3.cloned.1.call-update) | async-done | bytes 524304
  134.3 2.3 %fusion.8 = f32[32,1,1024]{2,1,0:T(1,128)} fusion(bf16[256,1,1024]{2,1,0:T(2,128)(2,1)} %all-reduce.3.cloned.1.call-done, u32[]{:T(128)S(6)} %multiply.1, f32[]{:T(128)} %psum.15), kind=kLoop, calls=%fused_computation.12 | loop fusion | flops 65536 | bytes 196616 | tf_op jit(solution)/shard_map/div | solution.py:60
  (3 shorter events, 0.0 us)
Async XLA Ops:
  7.2 7.0 %copy-start = (bf16[1,1,1024,1536]{3,2,1,0:T(8,128)(2,1)S(1)}, bf16[1,1,1024,1536]{3,2,1,0:T(8,128)(2,1)}, u32[]{:S(2)}) copy-start(bf16[1,1,1024,1536]{3,2,1,0:T(8,128)(2,1)} %param.7) | copy-start | bytes 9437188
  7.2 46.3 %reduce-scatter.2.cloned.1.call-start = ((), (), s32[]{:S(2)}) async-start(), calls=%async_computation.2 | async-start | bytes 2621440 | tf_op jit(solution)/shard_map/reduce_scatter | solution.py:21
  8.0 6.1 %copy-start.2 = (bf16[1536,32]{0,1:T(8,128)(2,1)S(1)}, bf16[1536,32]{0,1:T(8,128)(2,1)}, u32[]{:S(2)}) copy-start(bf16[1536,32]{0,1:T(8,128)(2,1)} %param.11) | copy-start | bytes 294916
  14.1 1.6 %copy-start.3 = (s32[1,1,1024]{2,1,0:T(1,128)S(1)}, s32[1,1,1024]{2,1,0:T(1,128)}, u32[]{:S(2)}) copy-start(s32[1,1,1024]{2,1,0:T(1,128)} %param.9) | copy-start | bytes 12292
  16.5 0.8 copy-start.1
  19.4 114.9 %all-reduce.3.cloned.1.call-start = ((), (), s32[]{:S(2)}) async-start(), calls=%async_computation.3 | async-start | bytes 2097152
  57.1 44.1 %copy-start.4 = (u32[256]{0:T(256)S(1)}, u32[256]{0:T(256)}, u32[]{:S(2)}) copy-start(u32[256]{0:T(256)} %constant.6) | copy-start | bytes 3076
  68.1 34.3 %all-to-all-start = ((bf16[8,2,16384]{2,1,0:T(2,128)(2,1)}), bf16[8,2,16384]{2,1,0:T(2,128)(2,1)}, u32[]{:S(2)}, u32[]{:S(2)}) async-start(bf16[8,2,16384]{2,1,0:T(2,128)(2,1)} %reshape.76), calls=%async_computation | async-start | bytes 1048576 | tf_op jit(solution)/shard_map/all_to_all | solution.py:55
Sparse Core Ops, SparseCore 0:
  19.5 33.9 reduce-scatter.1
  57.2 77.0 all-reduce.2
where the time goes:
time: 144 us; the launch traced here: 143 us
  waiting for transfers between devices  60.3 us (42%)
  blocking collectives  28.7 us (20%)
  local copies, waits for them, and re-layouts  16.2 us (11%)
  between operations  15.6 us (11%)
  matrix products  9.91 us (7%)
  other arithmetic  8.27 us (6%)
  starting transfers between devices  4.38 us (3%)
    reduce_scatter x1, waiting for transfers between devices, own_rows_2(): total = lax.psum_scatter(total, axis, scatter_dimension=0, tiled=True)  34.1 us
    psum x2, blocking collectives, over_axes(): return functools.reduce(lax.psum, axes, value)  28.7 us
    unnamed x3, waiting for transfers between devices  26.2 us
    unnamed x15, local copies, waits for them, and re-layouts  9.82 us
    dot_general x1, matrix products, body(): jnp.dot(inputs.reshape(experts * capacity, width), proj_in, preferred_ele...  6.06 us
    unnamed x1, other arithmetic  5.45 us
    all_to_all x1, starting transfers between devices, body(): lax.all_to_all(seq_grads, 'expert', split_axis=1, concat_axis=0, tiled=True)  4.3 us
    reduce_scatter x1, local copies, waits for them, and re-layouts, own_rows_2(): total = lax.psum_scatter(total, axis, scatter_dimension=0, tiled=True)  3.58 us
  transfers between devices with their start and end apart: 3, of which 2 were waited for; matrix products, arithmetic and copies ran while one was open for 12% of the time, Pallas kernels for 0%

commit v1 on v0

v1 whole, which is shorter than its diff:
```python
import functools

import jax
import jax.numpy as jnp
from jax import lax
from jax.experimental import pallas as pl
from jax.experimental.pallas import tpu as pltpu
from jax.sharding import Mesh
from jax.sharding import PartitionSpec as P

SEQ_DEV = 256
NX = 4
NZ = 8
K = 32
SQ = K * K
PANEL = SQ // NX
PIECE = PANEL // NZ
CAP = 1024
FAC = 72
ROWS = 256
VMEM_SPEC = pl.BlockSpec(memory_space=pltpu.VMEM)
SMEM_SPEC = pl.BlockSpec(memory_space=pltpu.SMEM)
NT = (((1,), (1,)), ((), ()))
TN = (((0,), (0,)), ((), ()))


def dot(a, b, dims):
    return lax.dot_general(a, b, dims, preferred_element_type=jnp.float32)


def project(cnt_ref, x_ref, g_ref, win_ref, wout_ref, seq_ref, fac_ref):
    i = pl.program_id(0)
    count = cnt_ref[0, 0]
    fac_ref[0:K, :] = dot(wout_ref[...], g_ref[...], NT).astype(jnp.bfloat16)
    fac_ref[K : 2 * K, :] = dot(win_ref[...], x_ref[...], NT).astype(jnp.bfloat16)
    slot = i * ROWS + lax.broadcasted_iota(jnp.int32, (8, ROWS), 1)
    row = lax.broadcasted_iota(jnp.int32, (8, ROWS), 0)
    seq = jnp.where(slot < count, jnp.broadcast_to(seq_ref[...], (8, ROWS)), SEQ_DEV)
    extra = jnp.where(row == 0, seq, jnp.where(row == 1, count >> 5, jnp.where(row == 2, count & 31, 0)))
    fac_ref[2 * K : FAC, :] = extra.astype(jnp.float32).astype(jnp.bfloat16)


def seq_grads(fac_ref, l_ref):
    seq = fac_ref[2 * K : FAC, :].astype(jnp.float32)[0:1, :]
    ids = lax.broadcasted_iota(jnp.int32, (SEQ_DEV, CAP), 0).astype(jnp.float32)
    onehot = jnp.where(ids == seq, 1.0, 0.0).astype(jnp.bfloat16)
    outs = fac_ref[0:K, :].astype(jnp.float32)
    ins = fac_ref[K : 2 * K, :].astype(jnp.float32)
    for c in range(NX):
        outer = jnp.concatenate(
            [(outs[k : k + 1, :] * ins).astype(jnp.bfloat16) for k in range(8 * c, 8 * c + 8)], axis=0
        )
        l_ref[:, c * PANEL : (c + 1) * PANEL] = dot(onehot, outer, NT).astype(jnp.bfloat16)


def panel_of(l_ref, x):
    mine = l_ref[:, pl.ds(pl.multiple_of(x * PANEL, PANEL), PANEL)]
    return dot(mine, l_ref[...], TN)


def own_part(x_ref, fac_ref, l_ref, p_ref):
    seq_grads(fac_ref, l_ref)
    p_ref[...] = panel_of(l_ref, x_ref[0])


def mid_part(x_ref, fa_ref, fb_ref, p0_ref, p_ref, l_ref):
    seq_grads(fa_ref, l_ref)
    acc = p0_ref[...] + panel_of(l_ref, x_ref[0])
    seq_grads(fb_ref, l_ref)
    p_ref[...] = acc + panel_of(l_ref, x_ref[0])


def last_part(x_ref, f0_ref, fa_ref, fb_ref, fc_ref, p1_ref, o_ref, l_ref):
    seq_grads(fc_ref, l_ref)
    total = p1_ref[...] + panel_of(l_ref, x_ref[0])
    for z in range(NZ):
        o_ref[z, :, 0:SQ] = total[z * PIECE : (z + 1) * PIECE, :].astype(jnp.bfloat16)
    extra = jnp.zeros((8, 128), jnp.float32)
    for ref in (f0_ref, fa_ref, fb_ref, fc_ref):
        extra = extra + ref[2 * K : FAC, 0:128].astype(jnp.float32)
    live = extra[1:2, :] * 32.0 + extra[2:3, :]
    high = jnp.floor(live * (1.0 / 64.0))
    low = live - high * 64.0
    row = lax.broadcasted_iota(jnp.int32, (PIECE, 128), 0)
    both = jnp.where(row == 0, high, jnp.where(row == 1, low, 0.0)).astype(jnp.bfloat16)
    for z in range(NZ):
        o_ref[z, :, SQ : SQ + 128] = both


def finish(r_ref, o_ref):
    total = jnp.zeros((PIECE, SQ + 128), jnp.float32)
    for z in range(NZ):
        total = total + r_ref[z].astype(jnp.float32)
    live = total[0:1, SQ : SQ + 1] * 64.0 + total[1:2, SQ : SQ + 1]
    o_ref[:, 0, :] = total[:, 0:SQ] / live


def shift(value, d):
    return lax.ppermute(value, "x", [(i, (i + d) % NX) for i in range(NX)])


def body(saved_inputs, saved_grads, row_counts, row_seq, proj_in, proj_out):
    width, ff = saved_inputs.shape[-1], saved_grads.shape[-1]
    x = lax.axis_index("x").astype(jnp.int32).reshape(1)
    fac = pl.pallas_call(
        project,
        grid=(CAP // ROWS,),
        in_specs=[
            SMEM_SPEC,
            pl.BlockSpec((ROWS, width), lambda i: (i, 0)),
            pl.BlockSpec((ROWS, ff), lambda i: (i, 0)),
            pl.BlockSpec((K, width), lambda i: (0, 0)),
            pl.BlockSpec((K, ff), lambda i: (0, 0)),
            pl.BlockSpec((1, ROWS), lambda i: (0, i)),
        ],
        out_specs=pl.BlockSpec((FAC, ROWS), lambda i: (0, i)),
        out_shape=jax.ShapeDtypeStruct((FAC, CAP), jnp.bfloat16),
        name="project",
    )(
        row_counts,
        saved_inputs.reshape(CAP, width),
        saved_grads.reshape(CAP, ff),
        proj_in.T,
        proj_out.T,
        row_seq.reshape(1, CAP),
    )
    far = shift(fac, 2)
    right = shift(fac, 1)
    left = shift(fac, 3)
    grads, part = pl.pallas_call(
        own_part,
        in_specs=[SMEM_SPEC, VMEM_SPEC],
        out_specs=[VMEM_SPEC, VMEM_SPEC],
        out_shape=[
            jax.ShapeDtypeStruct((SEQ_DEV, SQ), jnp.bfloat16),
            jax.ShapeDtypeStruct((PANEL, SQ), jnp.float32),
        ],
        name="own_part",
    )(x, fac)
    experts = lax.axis_size("expert")
    logged = lax.all_to_all(grads.reshape(experts, SEQ_DEV // experts, SQ), "expert", 0, 0, tiled=False)
    part = pl.pallas_call(
        mid_part,
        in_specs=[SMEM_SPEC] + [VMEM_SPEC] * 3,
        out_specs=VMEM_SPEC,
        out_shape=jax.ShapeDtypeStruct((PANEL, SQ), jnp.float32),
        scratch_shapes=[pltpu.VMEM((SEQ_DEV, SQ), jnp.bfloat16)],
        name="mid_part",
    )(x, right, left, part)
    pieces = pl.pallas_call(
        last_part,
        in_specs=[SMEM_SPEC] + [VMEM_SPEC] * 5,
        out_specs=VMEM_SPEC,
        out_shape=jax.ShapeDtypeStruct((NZ, PIECE, SQ + 128), jnp.bfloat16),
        scratch_shapes=[pltpu.VMEM((SEQ_DEV, SQ), jnp.bfloat16)],
        name="last_part",
    )(x, fac, right, left, far, part)
    got = lax.all_to_all(pieces, "z", 0, 0, tiled=False)
    fisher = pl.pallas_call(
        finish,
        in_specs=[VMEM_SPEC],
        out_specs=VMEM_SPEC,
        out_shape=jax.ShapeDtypeStruct((PIECE, 1, SQ), jnp.float32),
        name="finish",
    )(got)
    return (logged, fisher)


def solution(mesh):
    split = Mesh(mesh.devices.reshape(NX, NZ, mesh.shape["expert"]), ("x", "z", "expert"))
    dp = ("x", "z")
    in_specs = (
        P(dp, "expert", None, None),
        P(dp, "expert", None, None),
        P(dp, "expert"),
        P(dp, "expert", None),
        P(),
        P(),
    )
    out_specs = (P(None, ("x", "z", "expert"), None), P(dp, "expert", None))
    return jax.shard_map(body, mesh=split, in_specs=in_specs, out_specs=out_specs, check_vma=False)
```

time: 144 us -> 64.3 us (0.45)
  waiting for transfers between devices: 60.3 us -> 3.65 us
  Pallas kernels: 0 us -> 20.9 us
  between operations: 15.6 us -> 1.29 us
  local copies, waits for them, and re-layouts: 16.2 us -> 2.09 us
  matrix products: 9.91 us -> 0 us
  other arithmetic: 8.27 us -> 0 us
  starting transfers between devices: 4.38 us -> 8.62 us
  blocking collectives: 28.7 us -> 26.9 us
    reduce_scatter x1 -> x0, waiting for transfers between devices: 34.1 us -> none  [own_rows_2(): total = lax.psum_scatter(total, axis, scatter_dimension=0, tiled=True)]
    psum x2 -> x0, blocking collectives: 28.7 us -> none  [over_axes(): return functools.reduce(lax.psum, axes, value)]
    all_to_all x0 -> x1, blocking collectives: none -> 26.9 us  [body(): got = lax.all_to_all(pieces, 'z', 0, 0, tiled=False)]
    unnamed x3 -> x0, waiting for transfers between devices: 26.2 us -> none
    pallas_call x0 -> x5, Pallas kernels: none -> 20.9 us  [the longest x1 8.28 us: body(): pl.pallas_call(project, grid=(CAP // ROWS,), in_specs=[SMEM_SPEC, pl.Bloc...]
    dot_general x4 -> x0, matrix products: 9.91 us -> none  [the longest x1 6.06 us: body(): jnp.dot(inputs.reshape(experts * capacity, width), proj_in, preferred_ele...]
    unnamed x15 -> x7, local copies, waits for them, and re-layouts: 9.82 us -> 2.09 us
    unnamed x1 -> x0, other arithmetic: 5.45 us -> none
  transfers between devices with their start and end apart: 3 -> 4, of which waited for: 2 -> 2; matrix products, arithmetic and copies ran while one was open for 12% -> 0% of each run, Pallas kernels for 0% -> 12%
where the time goes in v1:
time: 64.3 us; the launch traced here: 63.4 us
  blocking collectives  26.9 us (42%)
  Pallas kernels  20.9 us (33%)
  starting transfers between devices  8.62 us (13%)
  waiting for transfers between devices  3.65 us (6%)
  local copies, waits for them, and re-layouts  2.09 us (3%)
  between operations  1.29 us (2%)
    all_to_all x1, blocking collectives, body(): got = lax.all_to_all(pieces, 'z', 0, 0, tiled=False)  26.9 us
    pallas_call x1, Pallas kernels, body(): pl.pallas_call(project, grid=(CAP // ROWS,), in_specs=[SMEM_SPEC, pl.Bloc...  8.28 us
    all_to_all x1, starting transfers between devices, body(): lax.all_to_all(grads.reshape(experts, SEQ_DEV // experts, SQ), 'expert',...  4.47 us
    pallas_call x1, Pallas kernels, body(): pl.pallas_call(mid_part, in_specs=[SMEM_SPEC] + [VMEM_SPEC] * 3, out_spec...  4.29 us
    ppermute x3, starting transfers between devices, shift(): return lax.ppermute(value, 'x', [(i, (i + d) % NX) for i in range(NX)])  4.14 us
    ppermute x3, waiting for transfers between devices, shift(): return lax.ppermute(value, 'x', [(i, (i + d) % NX) for i in range(NX)])  3.64 us
    pallas_call x1, Pallas kernels, body(): pl.pallas_call(last_part, in_specs=[SMEM_SPEC] + [VMEM_SPEC] * 5, out_spe...  3.45 us
    pallas_call x1, Pallas kernels, body(): pl.pallas_call(own_part, in_specs=[SMEM_SPEC, VMEM_SPEC], out_specs=[VMEM...  3.02 us
  transfers between devices with their start and end apart: 4, of which 2 were waited for; matrix products, arithmetic and copies ran while one was open for 0% of the time, Pallas kernels for 12%

profile of v1, /device:TPU:2, one launch (start us, length us, event | category | flops | bytes accessed | tf_op | source)
XLA Modules:
  0.0 63.4 jit_solution(5251691656872945937)
XLA Ops:
  1.3 8.3 %project.1.fac_ref.f0_ref = bf16[72,1024]{1,0:T(8,128)(2,1)} custom-call(s32[1,1]{1,0:T(1,128)S(6)} %copy.9.cnt_ref, bf16[1024,4096]{1,0:T(8,128)(2,1)} %bitcast.7, bf16[1024,1536]{1,0:T(8,128)(2,1)} %bitcast.8, bf16[32,4096]{1,0:T(8,128)(2,1)} %bitcast.10, bf16[32,1536]{1,0:T(8,128)(2,1)} %bitcast.11, s32[1,1024]{1,0:T(1,128)} %bitcast.12), custom_call_target="tpu_custom_call" | custom-call | tf_op jit(solution)/shard_map/project/pallas_call | solution.py:105
  9.6 3.0 %own_part.1 = (bf16[256,1024]{1,0:T(8,128)(2,1)}, f32[256,1024]{1,0:T(8,128)}) custom-call(s32[1]{0:T(128)} %bitcast.x_ref, bf16[72,1024]{1,0:T(8,128)(2,1)} %project.1.fac_ref.f0_ref), custom_call_target="tpu_custom_call" | custom-call | tf_op jit(solution)/shard_map/own_part/pallas_call | solution.py:130
  12.6 4.5 %all-to-all-start = ((bf16[8,32,1024]{2,1,0:T(8,128)(2,1)}), bf16[8,32,1024]{2,1,0:T(8,128)(2,1)S(1)}, u32[]{:S(2)}, u32[]{:S(2)}) async-start(bf16[8,32,1024]{2,1,0:T(8,128)(2,1)} %bitcast.9), calls=%async_computation | async-start | bytes 1048576 | tf_op jit(solution)/shard_map/all_to_all | solution.py:141
  17.1 1.5 %collective-permute-start = (bf16[72,1024]{1,0:T(8,128)(2,1)}, bf16[72,1024]{1,0:T(8,128)(2,1)S(1)}, u32[]{:S(2)}, u32[]{:S(2)}) collective-permute-start(bf16[72,1024]{1,0:T(8,128)(2,1)} %project.1.fac_ref.f0_ref), channel_id=1, source_target_pairs={{0,64},{64,128},{128,192},{192,0},{1,65},{65,129},{129,193},{193,1... | collective-permute-start | bytes 442376 | tf_op jit(solution)/shard_map/ppermute | solution.py:99
  18.5 0.5 collective-permute-start.1
  19.1 2.1 %collective-permute-start.2 = (bf16[72,1024]{1,0:T(8,128)(2,1)}, bf16[72,1024]{1,0:T(8,128)(2,1)S(1)}, u32[]{:S(2)}, u32[]{:S(2)}) collective-permute-start(bf16[72,1024]{1,0:T(8,128)(2,1)} %project.1.fac_ref.f0_ref), channel_id=1, source_target_pairs={{0,128},{64,192},{128,0},{192,64},{1,129},{65,193},{129,1},{193,65... | collective-permute-start | bytes 442376 | tf_op jit(solution)/shard_map/ppermute | solution.py:99
  21.2 2.5 %collective-permute-done.fa_ref = bf16[72,1024]{1,0:T(8,128)(2,1)S(1)} collective-permute-done((bf16[72,1024]{1,0:T(8,128)(2,1)}, bf16[72,1024]{1,0:T(8,128)(2,1)S(1)}, u32[]{:S(2)}, u32[]{:S(2)}) %collective-permute-start) | collective-permute-done | bytes 147488 | tf_op jit(solution)/shard_map/ppermute | solution.py:99
  23.7 0.0 copy-start
  23.7 1.2 %collective-permute-done.1.fb_ref = bf16[72,1024]{1,0:T(8,128)(2,1)S(1)} collective-permute-done((bf16[72,1024]{1,0:T(8,128)(2,1)}, bf16[72,1024]{1,0:T(8,128)(2,1)S(1)}, u32[]{:S(2)}, u32[]{:S(2)}) %collective-permute-start.1) | collective-permute-done | bytes 147488 | tf_op jit(solution)/shard_map/ppermute | solution.py:99
  24.8 0.0 copy-start.1
  24.8 0.0 copy-done
  24.9 0.6 %copy-done.1 = bf16[72,1024]{1,0:T(8,128)(2,1)} copy-done((bf16[72,1024]{1,0:T(8,128)(2,1)}, bf16[72,1024]{1,0:T(8,128)(2,1)S(1)}, u32[]{:S(2)}) %copy-start.1) | copy-done | bytes 147480
  25.5 4.3 %mid_part.1.p1_ref = f32[256,1024]{1,0:T(8,128)} custom-call(s32[1]{0:T(128)} %bitcast.x_ref, bf16[72,1024]{1,0:T(8,128)(2,1)} %copy-done, bf16[72,1024]{1,0:T(8,128)(2,1)} %copy-done.1, f32[256,1024]{1,0:T(8,128)} %get-tuple-element.5.p0_ref), custom_call_target="tpu_custom_call" | custom-call | tf_op jit(solution)/shard_map/mid_part/pallas_call | solution.py:142
  29.8 0.0 collective-permute-done.2.fc_ref
  29.8 0.0 copy-start.2
  29.8 0.6 %copy-done.2 = bf16[72,1024]{1,0:T(8,128)(2,1)} copy-done((bf16[72,1024]{1,0:T(8,128)(2,1)}, bf16[72,1024]{1,0:T(8,128)(2,1)S(1)}, u32[]{:S(2)}) %copy-start.2) | copy-done | bytes 147480
  30.4 3.5 %last_part.1 = bf16[8,32,1152]{2,1,0:T(8,128)(2,1)} custom-call(s32[1]{0:T(128)} %bitcast.x_ref, bf16[72,1024]{1,0:T(8,128)(2,1)} %project.1.fac_ref.f0_ref, bf16[72,1024]{1,0:T(8,128)(2,1)} %copy-done, bf16[72,1024]{1,0:T(8,128)(2,1)} %copy-done.1, bf16[72,1024]{1,0:T(8,128)(2,1)} %copy-done.2, f32[256,1024]{1,0:T(8,128)} %mid_part.1.p1_ref), custom_call_target="tpu_custom_call" | custom-call | tf_op jit(solution)/shard_map/last_part/pallas_call | solution.py:150
  33.9 0.0 all-to-all-done
  33.9 26.9 %all_to_all.10.r_ref = bf16[8,32,1152]{2,1,0:T(8,128)(2,1)} all-to-all(bf16[8,32,1152]{2,1,0:T(8,128)(2,1)} %last_part.1), channel_id=1, replica_groups=mesh['x'=4,'z'=8,'expert'=8] {'z'}, dimensions={0} | all-to-all | bytes 1179648 | tf_op jit(solution)/shard_map/all_to_all | solution.py:158
  60.8 1.8 %finish.1 = f32[32,1,1024]{2,1,0:T(1,128)} custom-call(bf16[8,32,1152]{2,1,0:T(8,128)(2,1)} %all_to_all.10.r_ref), custom_call_target="tpu_custom_call" | custom-call | tf_op jit(solution)/shard_map/finish/pallas_call | solution.py:159
  62.6 0.8 %copy.10 = bf16[8,32,1024]{2,1,0:T(8,128)(2,1)} copy(bf16[8,32,1024]{2,1,0:T(8,128)(2,1)S(1)} %all-to-all-done) | data formatting | bytes 1048576
Async XLA Ops:
  12.6 21.3 %all-to-all-start = ((bf16[8,32,1024]{2,1,0:T(8,128)(2,1)}), bf16[8,32,1024]{2,1,0:T(8,128)(2,1)S(1)}, u32[]{:S(2)}, u32[]{:S(2)}) async-start(bf16[8,32,1024]{2,1,0:T(8,128)(2,1)} %bitcast.9), calls=%async_computation | async-start | bytes 1048576 | tf_op jit(solution)/shard_map/all_to_all | solution.py:141
  17.1 6.6 %collective-permute-start = (bf16[72,1024]{1,0:T(8,128)(2,1)}, bf16[72,1024]{1,0:T(8,128)(2,1)S(1)}, u32[]{:S(2)}, u32[]{:S(2)}) collective-permute-start(bf16[72,1024]{1,0:T(8,128)(2,1)} %project.1.fac_ref.f0_ref), channel_id=1, source_target_pairs={{0,64},{64,128},{128,192},{192,0},{1,65},{65,129},{129,193},{193,1... | collective-permute-start | bytes 442376 | tf_op jit(solution)/shard_map/ppermute | solution.py:99
  18.5 6.3 %collective-permute-start.1 = (bf16[72,1024]{1,0:T(8,128)(2,1)}, bf16[72,1024]{1,0:T(8,128)(2,1)S(1)}, u32[]{:S(2)}, u32[]{:S(2)}) collective-permute-start(bf16[72,1024]{1,0:T(8,128)(2,1)} %project.1.fac_ref.f0_ref), channel_id=1, source_target_pairs={{0,192},{64,0},{128,64},{192,128},{1,193},{65,1},{129,65},{193,129... | collective-permute-start | bytes 442376 | tf_op jit(solution)/shard_map/ppermute | solution.py:99
  19.1 10.7 %collective-permute-start.2 = (bf16[72,1024]{1,0:T(8,128)(2,1)}, bf16[72,1024]{1,0:T(8,128)(2,1)S(1)}, u32[]{:S(2)}, u32[]{:S(2)}) collective-permute-start(bf16[72,1024]{1,0:T(8,128)(2,1)} %project.1.fac_ref.f0_ref), channel_id=1, source_target_pairs={{0,128},{64,192},{128,0},{192,64},{1,129},{65,193},{129,1},{193,65... | collective-permute-start | bytes 442376 | tf_op jit(solution)/shard_map/ppermute | solution.py:99
  23.7 1.2 %copy-start = (bf16[72,1024]{1,0:T(8,128)(2,1)}, bf16[72,1024]{1,0:T(8,128)(2,1)S(1)}, u32[]{:S(2)}) copy-start(bf16[72,1024]{1,0:T(8,128)(2,1)S(1)} %collective-permute-done.fa_ref) | copy-start | bytes 442372
  24.8 0.7 %copy-start.1 = (bf16[72,1024]{1,0:T(8,128)(2,1)}, bf16[72,1024]{1,0:T(8,128)(2,1)S(1)}, u32[]{:S(2)}) copy-start(bf16[72,1024]{1,0:T(8,128)(2,1)S(1)} %collective-permute-done.1.fb_ref) | copy-start | bytes 442372
  29.8 0.6 %copy-start.2 = (bf16[72,1024]{1,0:T(8,128)(2,1)}, bf16[72,1024]{1,0:T(8,128)(2,1)S(1)}, u32[]{:S(2)}) copy-start(bf16[72,1024]{1,0:T(8,128)(2,1)S(1)} %collective-permute-done.2.fc_ref) | copy-start | bytes 442372

commit v2 on v1

v2 whole, which is shorter than its diff:
```python
import jax
import jax.numpy as jnp
from jax import lax
from jax.experimental import pallas as pl
from jax.experimental.pallas import tpu as pltpu
from jax.sharding import Mesh
from jax.sharding import PartitionSpec as P


SEQ_DEV = 256
NX = 4
NZ = 8
K = 32
SQ = K * K
PANEL = SQ // NX
PIECE = PANEL // NZ
CAP = 1024
FAC = 72
CHUNKS = (
    (0, 0, 768),
    (0, 768, 768),
    (1, 0, 1024),
    (1, 1024, 1024),
    (1, 2048, 1024),
    (1, 3072, 512),
    (1, 3584, 512),
)
NSMALL = 2
MIB = 1 << 20
HBM_SPEC = pl.BlockSpec(memory_space=pltpu.MemorySpace.HBM)
SENT = (1, 6, 2, 5)
KEPT = (0, 7, 3, 4)
VMEM_SPEC = pl.BlockSpec(memory_space=pltpu.VMEM)
NT = (((1,), (1,)), ((), ()))
TN = (((0,), (0,)), ((), ()))


def dot(a, b, dims):
    return lax.dot_general(a, b, dims, preferred_element_type=jnp.float32)


def project(cnt_hbm, x_hbm, g_hbm, win_hbm, wout_hbm, seq_hbm, fac_ref, *scratch):
    cnt, win, wout, seq_row, sem, small = scratch[:6]
    parts = scratch[6:]
    first = [
        pltpu.make_async_copy(wout_hbm, wout, small.at[0]),
        pltpu.make_async_copy(win_hbm, win, small.at[1]),
        pltpu.make_async_copy(cnt_hbm, cnt, small.at[2]),
        pltpu.make_async_copy(seq_hbm, seq_row, small.at[3]),
    ]
    copies = []
    for i, (side, start, size) in enumerate(CHUNKS):
        source = (g_hbm, x_hbm)[side]
        copies.append(pltpu.make_async_copy(source.at[:, start : start + size], parts[i], sem.at[i]))
    first[0].start()
    copies[0].start()
    first[1].start()
    copies[1].start()
    first[2].start()
    first[3].start()
    for copy in copies[2:]:
        copy.start()
    sums = [None, None]
    first[0].wait()
    first[1].wait()
    for i, (side, start, size) in enumerate(CHUNKS):
        copies[i].wait()
        term = dot((wout, win)[side][:, start : start + size], parts[i][...], NT)
        sums[side] = term if sums[side] is None else sums[side] + term
        if i == NSMALL:
            first[2].wait()
            first[3].wait()
            count = cnt[0, 0]
            slot = lax.broadcasted_iota(jnp.int32, (8, CAP), 1)
            row = lax.broadcasted_iota(jnp.int32, (8, CAP), 0)
            seq = jnp.where(slot < count, jnp.broadcast_to(seq_row[...], (8, CAP)), SEQ_DEV)
            extra = jnp.where(row == 0, seq, jnp.where(row == 1, count >> 5, jnp.where(row == 2, count & 31, 0)))
            fac_ref[2 * K : FAC, :] = extra.astype(jnp.float32).astype(jnp.bfloat16)
            fac_ref[0:K, :] = sums[0].astype(jnp.bfloat16)
    fac_ref[K : 2 * K, :] = sums[1].astype(jnp.bfloat16)


def seq_grads(fac_ref, l_ref):
    seq = fac_ref[2 * K : FAC, :].astype(jnp.float32)[0:1, :]
    ids = lax.broadcasted_iota(jnp.int32, (SEQ_DEV, CAP), 0).astype(jnp.float32)
    onehot = jnp.where(ids == seq, 1.0, 0.0).astype(jnp.bfloat16)
    outs = fac_ref[0:K, :].astype(jnp.float32)
    ins = fac_ref[K : 2 * K, :].astype(jnp.float32)
    for c in range(NX):
        outer = jnp.concatenate(
            [(outs[k : k + 1, :] * ins).astype(jnp.bfloat16) for k in range(8 * c, 8 * c + 8)], axis=0
        )
        l_ref[:, c * PANEL : (c + 1) * PANEL] = dot(onehot, outer, NT).astype(jnp.bfloat16)


def panel_of(l_ref, x):
    mine = l_ref[:, pl.ds(pl.multiple_of(x * PANEL, PANEL), PANEL)]
    return dot(mine, l_ref[...], TN)


def own_part(fac_ref, l_ref, p_ref):
    seq_grads(fac_ref, l_ref)
    p_ref[...] = panel_of(l_ref, lax.axis_index("x"))


def mid_part(fa_ref, fb_ref, p0_ref, p_ref, l_ref):
    x = lax.axis_index("x")
    seq_grads(fa_ref, l_ref)
    acc = p0_ref[...] + panel_of(l_ref, x)
    seq_grads(fb_ref, l_ref)
    p_ref[...] = acc + panel_of(l_ref, x)


def last_part(f0_ref, fa_ref, fb_ref, fc_ref, p1_ref, sent_ref, kept_ref, l_ref, t_ref):
    x, z = lax.axis_index("x"), lax.axis_index("z")
    seq_grads(fc_ref, l_ref)
    t_ref[...] = p1_ref[...] + panel_of(l_ref, x)
    extra = jnp.zeros((8, 128), jnp.float32)
    for ref in (f0_ref, fa_ref, fb_ref, fc_ref):
        extra = extra + ref[2 * K : FAC, 0:128].astype(jnp.float32)
    live = extra[1:2, 0:1] * 32.0 + extra[2:3, 0:1]
    high = jnp.floor(live * (1.0 / 64.0))
    low = live - high * 64.0
    row = lax.broadcasted_iota(jnp.int32, (8, SQ), 0)
    lane = lax.broadcasted_iota(jnp.int32, (8, SQ), 1)
    for piece in range(NZ):
        rows = slice(piece * PIECE + PIECE - 8, (piece + 1) * PIECE)
        here = lane == (x * NZ + piece) * PIECE
        t_ref[rows, :] = jnp.where(here & (row == 7), high, jnp.where(here & (row == 6), low, t_ref[rows, :]))
    for ref, offsets in ((sent_ref, SENT), (kept_ref, KEPT)):
        for j, offset in enumerate(offsets):
            to = jnp.bitwise_xor(z, offset)
            rows = t_ref[pl.ds(pl.multiple_of(to * PIECE, PIECE), PIECE), :]
            ref[j] = rows.astype(ref.dtype)


def combine(kept_ref, got_ref, sent_ref, keep_ref):
    half = keep_ref.shape[0]
    for j in range(half):
        keep_ref[j] = kept_ref[j] + got_ref[j].astype(jnp.float32)
        sent_ref[j] = (kept_ref[half + j] + got_ref[half + j].astype(jnp.float32)).astype(jnp.bfloat16)


def finish(kept_ref, got_ref, o_ref):
    total = kept_ref[0] + got_ref[0].astype(jnp.float32)
    first = (lax.axis_index("x") * NZ + lax.axis_index("z")) * PIECE
    lane = lax.broadcasted_iota(jnp.int32, (1, SQ), 1)

    def pick(i, j):
        return jnp.sum(jnp.where(lane == first + j, total[i : i + 1, :], 0.0), axis=1, keepdims=True)

    live = pick(PIECE - 1, 0) * 64.0 + pick(PIECE - 2, 0)
    row = lax.broadcasted_iota(jnp.int32, (PIECE, SQ), 0)
    here = lax.broadcasted_iota(jnp.int32, (PIECE, SQ), 1) == first
    total = jnp.where(here & (row == PIECE - 1), pick(0, PIECE - 1), total)
    total = jnp.where(here & (row == PIECE - 2), pick(0, PIECE - 2), total)
    o_ref[:, 0, :] = total / live


def emit(l_ref, o_ref):
    o_ref[...] = l_ref[...]


def call(kernel, out, scratch=(), flops=0, vmem=14, in_specs=None, nin=0):
    return pl.pallas_call(
        kernel,
        in_specs=in_specs or [VMEM_SPEC] * nin,
        out_specs=[VMEM_SPEC] * len(out),
        out_shape=[jax.ShapeDtypeStruct(*o) for o in out],
        scratch_shapes=scratch,
        compiler_params=pltpu.CompilerParams(vmem_limit_bytes=vmem * MIB),
        cost_estimate=pl.CostEstimate(flops=flops, transcendentals=0, bytes_accessed=1 << 20),
    )


def shift(value, d):
    return lax.ppermute(value, "x", [(i, (i + d) % NX) for i in range(NX)])


def swap(value, d):
    return lax.ppermute(value, "z", [(i, i ^ d) for i in range(NZ)])


def step(saved_inputs, saved_grads, row_counts, row_seq, proj_in, proj_out):
    width, ff = saved_inputs.shape[-1], saved_grads.shape[-1]
    bf16, f32 = jnp.bfloat16, jnp.float32
    (fac,) = call(
        project,
        [((FAC, CAP), bf16)],
        [
            pltpu.SMEM((1, 1), jnp.int32),
            pltpu.VMEM((K, width), bf16),
            pltpu.VMEM((K, ff), bf16),
            pltpu.VMEM((1, CAP), jnp.int32),
            pltpu.SemaphoreType.DMA((len(CHUNKS),)),
            pltpu.SemaphoreType.DMA((4,)),
        ]
        + [pltpu.VMEM((CAP, size), bf16) for _, _, size in CHUNKS],
        in_specs=[HBM_SPEC] * 6,
        vmem=63,
    )(
        row_counts,
        saved_inputs.reshape(CAP, width),
        saved_grads.reshape(CAP, ff),
        proj_in.T,
        proj_out.T,
        row_seq.reshape(1, CAP),
    )
    far = shift(fac, 2)
    right = shift(fac, 1)
    left = shift(fac, 3)
    lbuf = pltpu.VMEM((SEQ_DEV, SQ), bf16)
    grads, part = call(own_part, [((SEQ_DEV, SQ), bf16), ((PANEL, SQ), f32)], nin=1, flops=1 << 30)(fac)
    experts = lax.axis_size("expert")
    logged = lax.all_to_all(grads.reshape(experts, SEQ_DEV // experts, SQ), "expert", 0, 0, tiled=False)
    (part,) = call(mid_part, [((PANEL, SQ), f32)], [lbuf], nin=3, flops=2 << 30)(right, left, part)
    sent, kept = call(
        last_part,
        [((4, PIECE, SQ), bf16), ((4, PIECE, SQ), f32)],
        [lbuf, pltpu.VMEM((PANEL, SQ), f32)],
        nin=5,
        flops=1 << 30,
    )(fac, right, left, far, part)
    got = swap(sent, 1)
    sent, kept = call(combine, [((2, PIECE, SQ), bf16), ((2, PIECE, SQ), f32)], nin=2)(kept, got)
    got = swap(sent, 3)
    sent, kept = call(combine, [((1, PIECE, SQ), bf16), ((1, PIECE, SQ), f32)], nin=2)(kept, got)
    got = swap(sent, 7)
    (logged,) = call(emit, [(logged.shape, bf16)], nin=1)(logged)
    (fisher,) = call(finish, [((PIECE, 1, SQ), f32)], nin=2)(kept, got)
    return (logged, fisher)


def solution(mesh):
    split = Mesh(mesh.devices.reshape(NX, NZ, mesh.shape["expert"]), ("x", "z", "expert"))
    dp = ("x", "z")
    in_specs = (
        P(dp, "expert", None, None),
        P(dp, "expert", None, None),
        P(dp, "expert"),
        P(dp, "expert", None),
        P(),
        P(),
    )
    out_specs = (P(None, ("x", "z", "expert"), None), P(dp, "expert", None))
    return jax.shard_map(step, mesh=split, in_specs=in_specs, out_specs=out_specs, check_vma=False)
```

time: 64.3 us -> 46.7 us (0.73)
  the two profiles are of different devices: /device:TPU:2 before, /device:TPU:46 now
where the time goes in v2:
time: 46.7 us; the launch traced here: 46.5 us
  starting transfers between devices  15.9 us (34%)
  Pallas kernels  14.2 us (30%)
  waiting for transfers between devices  14 us (30%)
  between operations  1.33 us (3%)
  local copies, waits for them, and re-layouts  0.95 us (2%)
    ppermute x3, waiting for transfers between devices, swap(): return lax.ppermute(value, 'z', [(i, i ^ d) for i in range(NZ)])  9.6 us
    pallas_call x1, Pallas kernels, step(): call(project, [((FAC, CAP), bf16)], [pltpu.SMEM((1, 1), jnp.int32), pltpu...  7.77 us
    ppermute x3, starting transfers between devices, swap(): return lax.ppermute(value, 'z', [(i, i ^ d) for i in range(NZ)])  7.52 us
    all_to_all x1, starting transfers between devices, step(): lax.all_to_all(grads.reshape(experts, SEQ_DEV // experts, SQ), 'expert',...  4.92 us
    ppermute x3, waiting for transfers between devices, shift(): return lax.ppermute(value, 'x', [(i, (i + d) % NX) for i in range(NX)])  4.41 us
    ppermute x3, starting transfers between devices, shift(): return lax.ppermute(value, 'x', [(i, (i + d) % NX) for i in range(NX)])  3.51 us
    pallas_call x1, Pallas kernels, step(): call(mid_part, [((PANEL, SQ), f32)], [lbuf], nin=3, flops=2 << 30)  1.98 us
    pallas_call x1, Pallas kernels, step(): call(own_part, [((SEQ_DEV, SQ), bf16), ((PANEL, SQ), f32)], nin=1, flops=...  1.58 us
  transfers between devices with their start and end apart: 7, of which 5 were waited for; matrix products, arithmetic and copies ran while one was open for 0% of the time, Pallas kernels for 10%

profile of v2, /device:TPU:46, one launch (start us, length us, event | category | flops | bytes accessed | tf_op | source)
XLA Modules:
  0.0 46.5 jit_solution(1475336542509524907)
XLA Ops:
  1.3 7.8 %shard_map.77.fac_ref.f0_ref = bf16[72,1024]{1,0:T(8,128)(2,1)} custom-call(s32[1,1]{1,0:T(1,128)S(6)} %copy.8.cnt_hbm, bf16[1024,4096]{1,0:T(8,128)(2,1)} %bitcast.6, bf16[1024,1536]{1,0:T(8,128)(2,1)} %bitcast.7, bf16[32,4096]{1,0:T(8,128)(2,1)} %bitcast.8, bf16[32,1536]{1,0:T(8,128)(2,1)} %bitcast.9, s32[1,1024]{1,0:T(1,128)} %bitcast.10), custom_call_target="tpu_custom_call" | custom-call | bytes 1048576 | tf_op jit(solution)/shard_map/pallas_call | solution.py:187
  9.1 0.6 %collective-permute-start = (bf16[72,1024]{1,0:T(8,128)(2,1)}, bf16[72,1024]{1,0:T(8,128)(2,1)S(1)}, u32[]{:S(2)}, u32[]{:S(2)}) collective-permute-start(bf16[72,1024]{1,0:T(8,128)(2,1)} %shard_map.77.fac_ref.f0_ref), channel_id=1, source_target_pairs={{0,64},{64,128},{128,192},{192,0},{1,65},{65,129},{129,193},{193,1... | collective-permute-start | bytes 442376 | tf_op jit(solution)/shard_map/ppermute | solution.py:177
  9.6 1.5 %collective-permute-start.1 = (bf16[72,1024]{1,0:T(8,128)(2,1)}, bf16[72,1024]{1,0:T(8,128)(2,1)S(1)}, u32[]{:S(2)}, u32[]{:S(2)}) collective-permute-start(bf16[72,1024]{1,0:T(8,128)(2,1)} %shard_map.77.fac_ref.f0_ref), channel_id=1, source_target_pairs={{0,192},{64,0},{128,64},{192,128},{1,193},{65,1},{129,65},{193,129... | collective-permute-start | bytes 442376 | tf_op jit(solution)/shard_map/ppermute | solution.py:177
  11.2 1.4 %collective-permute-start.2 = (bf16[72,1024]{1,0:T(8,128)(2,1)}, bf16[72,1024]{1,0:T(8,128)(2,1)S(1)}, u32[]{:S(2)}, u32[]{:S(2)}) collective-permute-start(bf16[72,1024]{1,0:T(8,128)(2,1)} %shard_map.77.fac_ref.f0_ref), channel_id=1, source_target_pairs={{0,128},{64,192},{128,0},{192,64},{1,129},{65,193},{129,1},{193,65... | collective-permute-start | bytes 442376 | tf_op jit(solution)/shard_map/ppermute | solution.py:177
  12.6 0.0 copy-start
  12.6 0.9 %copy-done = bf16[72,1024]{1,0:T(8,128)(2,1)S(1)} copy-done((bf16[72,1024]{1,0:T(8,128)(2,1)S(1)}, bf16[72,1024]{1,0:T(8,128)(2,1)}, u32[]{:S(2)}) %copy-start) | copy-done | bytes 147480
  13.5 0.0 copy-start.1
  13.5 1.6 %shard_map.78 = (bf16[256,1024]{1,0:T(8,128)(2,1)}, f32[256,1024]{1,0:T(8,128)S(1)}) custom-call(bf16[72,1024]{1,0:T(8,128)(2,1)S(1)} %copy-done), custom_call_target="tpu_custom_call" | custom-call | flops 1073741824 | bytes 1048576 | tf_op jit(solution)/shard_map/pallas_call | solution.py:213
  15.1 1.0 %collective-permute-done.fa_ref = bf16[72,1024]{1,0:T(8,128)(2,1)S(1)} collective-permute-done((bf16[72,1024]{1,0:T(8,128)(2,1)}, bf16[72,1024]{1,0:T(8,128)(2,1)S(1)}, u32[]{:S(2)}, u32[]{:S(2)}) %collective-permute-start) | collective-permute-done | bytes 147488 | tf_op jit(solution)/shard_map/ppermute | solution.py:177
  16.1 3.4 %collective-permute-done.1.fb_ref = bf16[72,1024]{1,0:T(8,128)(2,1)S(1)} collective-permute-done((bf16[72,1024]{1,0:T(8,128)(2,1)}, bf16[72,1024]{1,0:T(8,128)(2,1)S(1)}, u32[]{:S(2)}, u32[]{:S(2)}) %collective-permute-start.1) | collective-permute-done | bytes 147488 | tf_op jit(solution)/shard_map/ppermute | solution.py:177
  19.5 2.0 %shard_map.80.p1_ref = f32[256,1024]{1,0:T(8,128)S(1)} custom-call(bf16[72,1024]{1,0:T(8,128)(2,1)S(1)} %collective-permute-done.fa_ref, bf16[72,1024]{1,0:T(8,128)(2,1)S(1)} %collective-permute-done.1.fb_ref, f32[256,1024]{1,0:T(8,128)S(1)} %get-tuple-element.11.p0_ref), custom_call_target="tpu_custom_call" | custom-call | flops 2147483648 | bytes 1048576 | tf_op jit(solution)/shard_map/pallas_call | solution.py:216
  21.5 0.0 collective-permute-done.2.fc_ref
  21.5 0.0 copy-done.1
  21.5 1.2 %shard_map.81 = (bf16[4,32,1024]{2,1,0:T(8,128)(2,1)S(1)}, f32[4,32,1024]{2,1,0:T(8,128)S(1)}) custom-call(bf16[72,1024]{1,0:T(8,128)(2,1)S(1)} %copy-done.1, bf16[72,1024]{1,0:T(8,128)(2,1)S(1)} %collective-permute-done.fa_ref, bf16[72,1024]{1,0:T(8,128)(2,1)S(1)} %collective-permute-done.1.fb_ref, bf16[72,1024]{1,0:T(8,128)(2,1)S(1)} %collective-permute-done.2.fc_ref, ...), custom_call_target="tpu_custom_call" | custom-call | flops 1073741824 | bytes 1048576 | tf_op jit(solution)/shard_map/pallas_call | solution.py:217
  22.7 0.2 collective-permute-start.3
  22.9 4.9 %all-to-all-start = ((bf16[8,32,1024]{2,1,0:T(8,128)(2,1)}), bf16[8,32,1024]{2,1,0:T(8,128)(2,1)S(1)}, u32[]{:S(2)}, u32[]{:S(2)}) async-start(bf16[8,32,1024]{2,1,0:T(8,128)(2,1)} %bitcast.5), calls=%async_computation | async-start | bytes 1048576 | tf_op jit(solution)/shard_map/all_to_all | solution.py:215
  27.8 1.3 %collective-permute-done.3.got_ref = bf16[4,32,1024]{2,1,0:T(8,128)(2,1)S(1)} collective-permute-done((bf16[4,32,1024]{2,1,0:T(8,128)(2,1)S(1)}, bf16[4,32,1024]{2,1,0:T(8,128)(2,1)S(1)}, u32[]{:S(2)}, u32[]{:S(2)}) %collective-permute-start.3) | collective-permute-done | bytes 262176 | tf_op jit(solution)/shard_map/ppermute | solution.py:181
  29.2 2.5 %collective-permute-start.4 = (bf16[2,32,1024]{2,1,0:T(8,128)(2,1)S(1)}, bf16[2,32,1024]{2,1,0:T(8,128)(2,1)S(1)}, u32[]{:S(2)}, u32[]{:S(2)}) collective-permute-start(bf16[2,32,1024]{2,1,0:T(8,128)(2,1)S(1)} %get-tuple-element.15), channel_id=1, source_target_pairs={{0,24},{8,16},{16,8},{24,0},{32,56},{40,48},{48,40},{56,32},{1,25}... | collective-permute-start | bytes 393224 | tf_op jit(solution)/shard_map/ppermute | solution.py:181
  31.7 6.6 %collective-permute-done.4.got_ref = bf16[2,32,1024]{2,1,0:T(8,128)(2,1)S(1)} collective-permute-done((bf16[2,32,1024]{2,1,0:T(8,128)(2,1)S(1)}, bf16[2,32,1024]{2,1,0:T(8,128)(2,1)S(1)}, u32[]{:S(2)}, u32[]{:S(2)}) %collective-permute-start.4) | collective-permute-done | bytes 131104 | tf_op jit(solution)/shard_map/ppermute | solution.py:181
  38.3 4.9 %collective-permute-start.5 = (bf16[1,32,1024]{2,1,0:T(8,128)(2,1)S(1)}, bf16[1,32,1024]{2,1,0:T(8,128)(2,1)S(1)}, u32[]{:S(2)}, u32[]{:S(2)}) collective-permute-start(bf16[1,32,1024]{2,1,0:T(8,128)(2,1)S(1)} %get-tuple-element.17), channel_id=1, source_target_pairs={{0,56},{8,48},{16,40},{24,32},{32,24},{40,16},{48,8},{56,0},{1,57}... | collective-permute-start | bytes 196616 | tf_op jit(solution)/shard_map/ppermute | solution.py:181
  43.1 0.0 all-to-all-done.l_ref
  43.1 0.8 %shard_map.79 = bf16[8,32,1024]{2,1,0:T(8,128)(2,1)} custom-call(bf16[8,32,1024]{2,1,0:T(8,128)(2,1)S(1)} %all-to-all-done.l_ref), custom_call_target="tpu_custom_call" | custom-call | bytes 1048576 | tf_op jit(solution)/shard_map/pallas_call | solution.py:229
  44.0 1.7 %collective-permute-done.5.got_ref = bf16[1,32,1024]{2,1,0:T(8,128)(2,1)S(1)} collective-permute-done((bf16[1,32,1024]{2,1,0:T(8,128)(2,1)S(1)}, bf16[1,32,1024]{2,1,0:T(8,128)(2,1)S(1)}, u32[]{:S(2)}, u32[]{:S(2)}) %collective-permute-start.5) | collective-permute-done | bytes 65568 | tf_op jit(solution)/shard_map/ppermute | solution.py:181
  45.6 0.8 %shard_map.84 = f32[32,1,1024]{2,1,0:T(1,128)} custom-call(f32[1,32,1024]{2,1,0:T(8,128)S(1)} %get-tuple-element.16.kept_ref, bf16[1,32,1024]{2,1,0:T(8,128)(2,1)S(1)} %collective-permute-done.5.got_ref), custom_call_target="tpu_custom_call" | custom-call | bytes 1048576 | tf_op jit(solution)/shard_map/pallas_call | solution.py:230
  (2 shorter events, 0.1 us)
Async XLA Ops:
  9.1 7.0 %collective-permute-start = (bf16[72,1024]{1,0:T(8,128)(2,1)}, bf16[72,1024]{1,0:T(8,128)(2,1)S(1)}, u32[]{:S(2)}, u32[]{:S(2)}) collective-permute-start(bf16[72,1024]{1,0:T(8,128)(2,1)} %shard_map.77.fac_ref.f0_ref), channel_id=1, source_target_pairs={{0,64},{64,128},{128,192},{192,0},{1,65},{65,129},{129,193},{193,1... | collective-permute-start | bytes 442376 | tf_op jit(solution)/shard_map/ppermute | solution.py:177
  9.6 9.9 %collective-permute-start.1 = (bf16[72,1024]{1,0:T(8,128)(2,1)}, bf16[72,1024]{1,0:T(8,128)(2,1)S(1)}, u32[]{:S(2)}, u32[]{:S(2)}) collective-permute-start(bf16[72,1024]{1,0:T(8,128)(2,1)} %shard_map.77.fac_ref.f0_ref), channel_id=1, source_target_pairs={{0,192},{64,0},{128,64},{192,128},{1,193},{65,1},{129,65},{193,129... | collective-permute-start | bytes 442376 | tf_op jit(solution)/shard_map/ppermute | solution.py:177
  11.2 10.3 %collective-permute-start.2 = (bf16[72,1024]{1,0:T(8,128)(2,1)}, bf16[72,1024]{1,0:T(8,128)(2,1)S(1)}, u32[]{:S(2)}, u32[]{:S(2)}) collective-permute-start(bf16[72,1024]{1,0:T(8,128)(2,1)} %shard_map.77.fac_ref.f0_ref), channel_id=1, source_target_pairs={{0,128},{64,192},{128,0},{192,64},{1,129},{65,193},{129,1},{193,65... | collective-permute-start | bytes 442376 | tf_op jit(solution)/shard_map/ppermute | solution.py:177
  12.6 0.9 %copy-start = (bf16[72,1024]{1,0:T(8,128)(2,1)S(1)}, bf16[72,1024]{1,0:T(8,128)(2,1)}, u32[]{:S(2)}) copy-start(bf16[72,1024]{1,0:T(8,128)(2,1)} %shard_map.77.fac_ref.f0_ref) | copy-start | bytes 442372
  13.5 8.0 %copy-start.1 = (bf16[72,1024]{1,0:T(8,128)(2,1)S(1)}, bf16[72,1024]{1,0:T(8,128)(2,1)}, u32[]{:S(2)}) copy-start(bf16[72,1024]{1,0:T(8,128)(2,1)} %shard_map.77.fac_ref.f0_ref) | copy-start | bytes 442372
  22.7 6.5 %collective-permute-start.3 = (bf16[4,32,1024]{2,1,0:T(8,128)(2,1)S(1)}, bf16[4,32,1024]{2,1,0:T(8,128)(2,1)S(1)}, u32[]{:S(2)}, u32[]{:S(2)}) collective-permute-start(bf16[4,32,1024]{2,1,0:T(8,128)(2,1)S(1)} %get-tuple-element.13), channel_id=1, source_target_pairs={{0,8},{8,0},{16,24},{24,16},{32,40},{40,32},{48,56},{56,48},{1,9},... | collective-permute-start | bytes 786440 | tf_op jit(solution)/shard_map/ppermute | solution.py:181
  22.9 20.3 %all-to-all-start = ((bf16[8,32,1024]{2,1,0:T(8,128)(2,1)}), bf16[8,32,1024]{2,1,0:T(8,128)(2,1)S(1)}, u32[]{:S(2)}, u32[]{:S(2)}) async-start(bf16[8,32,1024]{2,1,0:T(8,128)(2,1)} %bitcast.5), calls=%async_computation | async-start | bytes 1048576 | tf_op jit(solution)/shard_map/all_to_all | solution.py:215
  29.2 9.1 %collective-permute-start.4 = (bf16[2,32,1024]{2,1,0:T(8,128)(2,1)S(1)}, bf16[2,32,1024]{2,1,0:T(8,128)(2,1)S(1)}, u32[]{:S(2)}, u32[]{:S(2)}) collective-permute-start(bf16[2,32,1024]{2,1,0:T(8,128)(2,1)S(1)} %get-tuple-element.15), channel_id=1, source_target_pairs={{0,24},{8,16},{16,8},{24,0},{32,56},{40,48},{48,40},{56,32},{1,25}... | collective-permute-start | bytes 393224 | tf_op jit(solution)/shard_map/ppermute | solution.py:181
  38.3 7.4 %collective-permute-start.5 = (bf16[1,32,1024]{2,1,0:T(8,128)(2,1)S(1)}, bf16[1,32,1024]{2,1,0:T(8,128)(2,1)S(1)}, u32[]{:S(2)}, u32[]{:S(2)}) collective-permute-start(bf16[1,32,1024]{2,1,0:T(8,128)(2,1)S(1)} %get-tuple-element.17), channel_id=1, source_target_pairs={{0,56},{8,48},{16,40},{24,32},{32,24},{40,16},{48,8},{56,0},{1,57}... | collective-permute-start | bytes 196616 | tf_op jit(solution)/shard_map/ppermute | solution.py:181

commit v3 on v2

--- a/solution.py
+++ b/solution.py
@@ -16,20 +16,10 @@
 PIECE = PANEL // NZ
 CAP = 1024
 FAC = 72
-CHUNKS = (
-    (0, 0, 768),
-    (0, 768, 768),
-    (1, 0, 1024),
-    (1, 1024, 1024),
-    (1, 2048, 1024),
-    (1, 3072, 512),
-    (1, 3584, 512),
-)
-NSMALL = 2
+HALF_CAP = CAP // 2
 MIB = 1 << 20
 HBM_SPEC = pl.BlockSpec(memory_space=pltpu.MemorySpace.HBM)
-SENT = (1, 6, 2, 5)
-KEPT = (0, 7, 3, 4)
+ROUNDS = (1, 7, 3)
 VMEM_SPEC = pl.BlockSpec(memory_space=pltpu.VMEM)
 NT = (((1,), (1,)), ((), ()))
 TN = (((0,), (0,)), ((), ()))
@@ -39,45 +29,35 @@
     return lax.dot_general(a, b, dims, preferred_element_type=jnp.float32)
 
 
-def project(cnt_hbm, x_hbm, g_hbm, win_hbm, wout_hbm, seq_hbm, fac_ref, *scratch):
-    cnt, win, wout, seq_row, sem, small = scratch[:6]
-    parts = scratch[6:]
-    first = [
-        pltpu.make_async_copy(wout_hbm, wout, small.at[0]),
-        pltpu.make_async_copy(win_hbm, win, small.at[1]),
-        pltpu.make_async_copy(cnt_hbm, cnt, small.at[2]),
-        pltpu.make_async_copy(seq_hbm, seq_row, small.at[3]),
-    ]
-    copies = []
-    for i, (side, start, size) in enumerate(CHUNKS):
-        source = (g_hbm, x_hbm)[side]
-        copies.append(pltpu.make_async_copy(source.at[:, start : start + size], parts[i], sem.at[i]))
-    first[0].start()
-    copies[0].start()
-    first[1].start()
-    copies[1].start()
-    first[2].start()
-    first[3].start()
-    for copy in copies[2:]:
-        copy.start()
-    sums = [None, None]
-    first[0].wait()
-    first[1].wait()
-    for i, (side, start, size) in enumerate(CHUNKS):
-        copies[i].wait()
-        term = dot((wout, win)[side][:, start : start + size], parts[i][...], NT)
-        sums[side] = term if sums[side] is None else sums[side] + term
-        if i == NSMALL:
-            first[2].wait()
-            first[3].wait()
-            count = cnt[0, 0]
-            slot = lax.broadcasted_iota(jnp.int32, (8, CAP), 1)
-            row = lax.broadcasted_iota(jnp.int32, (8, CAP), 0)
-            seq = jnp.where(slot < count, jnp.broadcast_to(seq_row[...], (8, CAP)), SEQ_DEV)
-            extra = jnp.where(row == 0, seq, jnp.where(row == 1, count >> 5, jnp.where(row == 2, count & 31, 0)))
-            fac_ref[2 * K : FAC, :] = extra.astype(jnp.float32).astype(jnp.bfloat16)
-            fac_ref[0:K, :] = sums[0].astype(jnp.bfloat16)
-    fac_ref[K : 2 * K, :] = sums[1].astype(jnp.bfloat16)
+def project(cnt_ref, x_hbm, g_hbm, win_hbm, wout_hbm, seq_hbm, fac_ref, win, wout, seq_row, x0, x1, g, sem):
+    low, high = slice(0, HALF_CAP), slice(HALF_CAP, CAP)
+    copy_win = pltpu.make_async_copy(win_hbm, win, sem.at[0])
+    copy_wout = pltpu.make_async_copy(wout_hbm, wout, sem.at[1])
+    copy_seq = pltpu.make_async_copy(seq_hbm, seq_row, sem.at[2])
+    copy_x0 = pltpu.make_async_copy(x_hbm.at[low], x0, sem.at[3])
+    copy_x1 = pltpu.make_async_copy(x_hbm.at[high], x1, sem.at[4])
+    copy_g = pltpu.make_async_copy(g_hbm, g, sem.at[5])
+    copy_win.start()
+    copy_x0.start()
+    copy_x1.start()
+    copy_wout.start()
+    copy_seq.start()
+    copy_win.wait()
+    copy_x0.wait()
+    copy_g.start()
+    fac_ref[K : 2 * K, low] = dot(win[...], x0[...], NT).astype(jnp.bfloat16)
+    copy_seq.wait()
+    count = jnp.broadcast_to(cnt_ref[...], (8, CAP))
+    slot = lax.broadcasted_iota(jnp.int32, (8, CAP), 1)
+    row = lax.broadcasted_iota(jnp.int32, (8, CAP), 0)
+    seq = jnp.where(slot < count, jnp.broadcast_to(seq_row[...], (8, CAP)), SEQ_DEV)
+    extra = jnp.where(row == 0, seq, jnp.where(row == 1, count >> 5, jnp.where(row == 2, count & 31, 0)))
+    fac_ref[2 * K : FAC, :] = extra.astype(jnp.float32).astype(jnp.bfloat16)
+    copy_x1.wait()
+    fac_ref[K : 2 * K, high] = dot(win[...], x1[...], NT).astype(jnp.bfloat16)
+    copy_wout.wait()
+    copy_g.wait()
+    fac_ref[0:K, :] = dot(wout[...], g[...], NT).astype(jnp.bfloat16)
 
 
 def seq_grads(fac_ref, l_ref):
@@ -109,6 +89,10 @@
     acc = p0_ref[...] + panel_of(l_ref, x)
     seq_grads(fb_ref, l_ref)
     p_ref[...] = acc + panel_of(l_ref, x)
+
+
+def hop(z, d):
+    return lax.rem(z + jnp.where(lax.rem(z, 2) == 0, d, NZ - d), NZ)
 
 
 def last_part(f0_ref, fa_ref, fb_ref, fc_ref, p1_ref, sent_ref, kept_ref, l_ref, t_ref):
@@ -127,10 +111,14 @@
         rows = slice(piece * PIECE + PIECE - 8, (piece + 1) * PIECE)
         here = lane == (x * NZ + piece) * PIECE
         t_ref[rows, :] = jnp.where(here & (row == 7), high, jnp.where(here & (row == 6), low, t_ref[rows, :]))
-    for ref, offsets in ((sent_ref, SENT), (kept_ref, KEPT)):
-        for j, offset in enumerate(offsets):
-            to = jnp.bitwise_xor(z, offset)
-            rows = t_ref[pl.ds(pl.multiple_of(to * PIECE, PIECE), PIECE), :]
+    first, second, third = ROUNDS
+    to = hop(z, first)
+    for ref, order in (
+        (sent_ref, (to, hop(to, third), hop(to, second), hop(hop(to, second), third))),
+        (kept_ref, (z, hop(z, third), hop(z, second), hop(hop(z, second), third))),
+    ):
+        for j, piece in enumerate(order):
+            rows = t_ref[pl.ds(pl.multiple_of(piece * PIECE, PIECE), PIECE), :]
             ref[j] = rows.astype(ref.dtype)
 
 
@@ -178,7 +166,8 @@
 
 
 def swap(value, d):
-    return lax.ppermute(value, "z", [(i, i ^ d) for i in range(NZ)])
+    pairs = [(i, (i + (d if i % 2 == 0 else NZ - d)) % NZ) for i in range(NZ)]
+    return lax.ppermute(value, "z", pairs)
 
 
 def step(saved_inputs, saved_grads, row_counts, row_seq, proj_in, proj_out):
@@ -188,23 +177,28 @@
         project,
         [((FAC, CAP), bf16)],
         [
-            pltpu.SMEM((1, 1), jnp.int32),
             pltpu.VMEM((K, width), bf16),
             pltpu.VMEM((K, ff), bf16),
             pltpu.VMEM((1, CAP), jnp.int32),
-            pltpu.SemaphoreType.DMA((len(CHUNKS),)),
-            pltpu.SemaphoreType.DMA((4,)),
-        ]
-        + [pltpu.VMEM((CAP, size), bf16) for _, _, size in CHUNKS],
-        in_specs=[HBM_SPEC] * 6,
-        vmem=63,
+            pltpu.VMEM((HALF_CAP, width), bf16),
+            pltpu.VMEM((HALF_CAP, width), bf16),
+            pltpu.VMEM((CAP, ff), bf16),
+            pltpu.SemaphoreType.DMA((6,)),
+        ],
+        in_specs=[VMEM_SPEC] + [HBM_SPEC] * 5,
+        vmem=24,
     )(
         row_counts,
-        saved_inputs.reshape(CAP, width),
-        saved_grads.reshape(CAP, ff),
-        proj_in.T,
-        proj_out.T,
-        row_seq.reshape(1, CAP),
+        *(
+            pltpu.with_memory_space_constraint(value, pltpu.MemorySpace.HBM)
+            for value in (
+                saved_inputs.reshape(CAP, width),
+                saved_grads.reshape(CAP, ff),
+                proj_in.T,
+                proj_out.T,
+                row_seq.reshape(1, CAP),
+            )
+        ),
     )
     far = shift(fac, 2)
     right = shift(fac, 1)
@@ -223,9 +217,9 @@
     )(fac, right, left, far, part)
     got = swap(sent, 1)
     sent, kept = call(combine, [((2, PIECE, SQ), bf16), ((2, PIECE, SQ), f32)], nin=2)(kept, got)
+    got = swap(sent, 7)
+    sent, kept = call(combine, [((1, PIECE, SQ), bf16), ((1, PIECE, SQ), f32)], nin=2)(kept, got)
     got = swap(sent, 3)
-    sent, kept = call(combine, [((1, PIECE, SQ), bf16), ((1, PIECE, SQ), f32)], nin=2)(kept, got)
-    got = swap(sent, 7)
     (logged,) = call(emit, [(logged.shape, bf16)], nin=1)(logged)
     (fisher,) = call(finish, [((PIECE, 1, SQ), f32)], nin=2)(kept, got)
     return (logged, fisher)

time: 46.7 us -> 43.9 us (0.940)
  the two profiles are of different devices: /device:TPU:46 before, /device:TPU:6 now
where the time goes in v3:
time: 43.9 us; the launch traced here: 43.7 us
  starting transfers between devices  16.7 us (38%)
  waiting for transfers between devices  13.1 us (30%)
  Pallas kernels  12.6 us (29%)
  between operations  1.32 us (3%)
    ppermute x3, starting transfers between devices, swap(): return lax.ppermute(value, 'z', pairs)  8.41 us
    ppermute x3, waiting for transfers between devices, swap(): return lax.ppermute(value, 'z', pairs)  7.53 us
    pallas_call x1, Pallas kernels, step(): call(project, [((FAC, CAP), bf16)], [pltpu.VMEM((K, width), bf16), pltpu....  6.13 us
    ppermute x3, waiting for transfers between devices, shift(): return lax.ppermute(value, 'x', [(i, (i + d) % NX) for i in range(NX)])  5.6 us
    all_to_all x1, starting transfers between devices, step(): lax.all_to_all(grads.reshape(experts, SEQ_DEV // experts, SQ), 'expert',...  4.47 us
    ppermute x3, starting transfers between devices, shift(): return lax.ppermute(value, 'x', [(i, (i + d) % NX) for i in range(NX)])  3.82 us
    pallas_call x1, Pallas kernels, step(): call(mid_part, [((PANEL, SQ), f32)], [lbuf], nin=3, flops=2 << 30)  1.98 us
    pallas_call x1, Pallas kernels, step(): call(own_part, [((SEQ_DEV, SQ), bf16), ((PANEL, SQ), f32)], nin=1, flops=...  1.58 us
  transfers between devices with their start and end apart: 7, of which 5 were waited for; matrix products, arithmetic and copies ran while one was open for 0% of the time, Pallas kernels for 10%

profile of v3, /device:TPU:6, one launch (start us, length us, event | category | flops | bytes accessed | tf_op | source)
XLA Modules:
  0.0 43.7 jit_solution(18162262230169914191)
XLA Ops:
  1.3 6.1 %shard_map.77.fac_ref.f0_ref = bf16[72,1024]{1,0:T(8,128)(2,1)S(1)} custom-call(s32[1,1]{1,0:T(1,128)S(6)} %copy.8.cnt_ref, bf16[1024,4096]{1,0:T(8,128)(2,1)} %bitcast.6, bf16[1024,1536]{1,0:T(8,128)(2,1)} %bitcast.7, bf16[32,4096]{1,0:T(8,128)(2,1)} %bitcast.8, bf16[32,1536]{1,0:T(8,128)(2,1)} %bitcast.9, s32[1,1024]{1,0:T(1,128)} %bitcast.10), custom_call_target="tpu_custom_call" | custom-call | bytes 1048576 | tf_op jit(solution)/shard_map/pallas_call | solution.py:176
  7.4 2.3 %collective-permute-start = (bf16[72,1024]{1,0:T(8,128)(2,1)S(1)}, bf16[72,1024]{1,0:T(8,128)(2,1)S(1)}, u32[]{:S(2)}, u32[]{:S(2)}) collective-permute-start(bf16[72,1024]{1,0:T(8,128)(2,1)S(1)} %shard_map.77.fac_ref.f0_ref), channel_id=1, source_target_pairs={{0,64},{64,128},{128,192},{192,0},{1,65},{65,129},{129,193},{193,1... | collective-permute-start | bytes 442376 | tf_op jit(solution)/shard_map/ppermute | solution.py:165
  9.7 0.0 collective-permute-start.1
  9.7 1.6 %collective-permute-start.2 = (bf16[72,1024]{1,0:T(8,128)(2,1)S(1)}, bf16[72,1024]{1,0:T(8,128)(2,1)S(1)}, u32[]{:S(2)}, u32[]{:S(2)}) collective-permute-start(bf16[72,1024]{1,0:T(8,128)(2,1)S(1)} %shard_map.77.fac_ref.f0_ref), channel_id=1, source_target_pairs={{0,128},{64,192},{128,0},{192,64},{1,129},{65,193},{129,1},{193,65... | collective-permute-start | bytes 442376 | tf_op jit(solution)/shard_map/ppermute | solution.py:165
  11.2 1.6 %shard_map.78 = (bf16[256,1024]{1,0:T(8,128)(2,1)}, f32[256,1024]{1,0:T(8,128)S(1)}) custom-call(bf16[72,1024]{1,0:T(8,128)(2,1)S(1)} %shard_map.77.fac_ref.f0_ref), custom_call_target="tpu_custom_call" | custom-call | flops 1073741824 | bytes 1048576 | tf_op jit(solution)/shard_map/pallas_call | solution.py:207
  12.8 1.4 %collective-permute-done.fa_ref = bf16[72,1024]{1,0:T(8,128)(2,1)S(1)} collective-permute-done((bf16[72,1024]{1,0:T(8,128)(2,1)S(1)}, bf16[72,1024]{1,0:T(8,128)(2,1)S(1)}, u32[]{:S(2)}, u32[]{:S(2)}) %collective-permute-start) | collective-permute-done | bytes 147488 | tf_op jit(solution)/shard_map/ppermute | solution.py:165
  14.2 4.2 %collective-permute-done.1.fb_ref = bf16[72,1024]{1,0:T(8,128)(2,1)S(1)} collective-permute-done((bf16[72,1024]{1,0:T(8,128)(2,1)S(1)}, bf16[72,1024]{1,0:T(8,128)(2,1)S(1)}, u32[]{:S(2)}, u32[]{:S(2)}) %collective-permute-start.1) | collective-permute-done | bytes 147488 | tf_op jit(solution)/shard_map/ppermute | solution.py:165
  18.4 2.0 %shard_map.80.p1_ref = f32[256,1024]{1,0:T(8,128)S(1)} custom-call(bf16[72,1024]{1,0:T(8,128)(2,1)S(1)} %collective-permute-done.fa_ref, bf16[72,1024]{1,0:T(8,128)(2,1)S(1)} %collective-permute-done.1.fb_ref, f32[256,1024]{1,0:T(8,128)S(1)} %get-tuple-element.11.p0_ref), custom_call_target="tpu_custom_call" | custom-call | flops 2147483648 | bytes 1048576 | tf_op jit(solution)/shard_map/pallas_call | solution.py:210
  20.4 0.0 collective-permute-done.2.fc_ref
  20.4 1.2 %shard_map.81 = (bf16[4,32,1024]{2,1,0:T(8,128)(2,1)S(1)}, f32[4,32,1024]{2,1,0:T(8,128)S(1)}) custom-call(bf16[72,1024]{1,0:T(8,128)(2,1)S(1)} %shard_map.77.fac_ref.f0_ref, bf16[72,1024]{1,0:T(8,128)(2,1)S(1)} %collective-permute-done.fa_ref, bf16[72,1024]{1,0:T(8,128)(2,1)S(1)} %collective-permute-done.1.fb_ref, ...), custom_call_target="tpu_custom_call" | custom-call | flops 1073741824 | bytes 1048576 | tf_op jit(solution)/shard_map/pallas_call | solution.py:211
  21.6 1.2 %collective-permute-start.3 = (bf16[4,32,1024]{2,1,0:T(8,128)(2,1)S(1)}, bf16[4,32,1024]{2,1,0:T(8,128)(2,1)S(1)}, u32[]{:S(2)}, u32[]{:S(2)}) collective-permute-start(bf16[4,32,1024]{2,1,0:T(8,128)(2,1)S(1)} %get-tuple-element.13), channel_id=1, source_target_pairs={{0,8},{8,0},{16,24},{24,16},{32,40},{40,32},{48,56},{56,48},{1,9},... | collective-permute-start | bytes 786440 | tf_op jit(solution)/shard_map/ppermute | solution.py:170
  22.8 4.5 %all-to-all-start = ((bf16[8,32,1024]{2,1,0:T(8,128)(2,1)}), bf16[8,32,1024]{2,1,0:T(8,128)(2,1)S(1)}, u32[]{:S(2)}, u32[]{:S(2)}) async-start(bf16[8,32,1024]{2,1,0:T(8,128)(2,1)} %bitcast.5), calls=%async_computation | async-start | bytes 1048576 | tf_op jit(solution)/shard_map/all_to_all | solution.py:209
  27.3 0.8 %collective-permute-done.3.got_ref = bf16[4,32,1024]{2,1,0:T(8,128)(2,1)S(1)} collective-permute-done((bf16[4,32,1024]{2,1,0:T(8,128)(2,1)S(1)}, bf16[4,32,1024]{2,1,0:T(8,128)(2,1)S(1)}, u32[]{:S(2)}, u32[]{:S(2)}) %collective-permute-start.3) | collective-permute-done | bytes 262176 | tf_op jit(solution)/shard_map/ppermute | solution.py:170
  28.1 5.2 %collective-permute-start.4 = (bf16[2,32,1024]{2,1,0:T(8,128)(2,1)S(1)}, bf16[2,32,1024]{2,1,0:T(8,128)(2,1)S(1)}, u32[]{:S(2)}, u32[]{:S(2)}) collective-permute-start(bf16[2,32,1024]{2,1,0:T(8,128)(2,1)S(1)} %get-tuple-element.15), channel_id=1, source_target_pairs={{0,56},{8,16},{16,8},{24,32},{32,24},{40,48},{48,40},{56,0},{1,57}... | collective-permute-start | bytes 393224 | tf_op jit(solution)/shard_map/ppermute | solution.py:170
  33.3 3.3 %collective-permute-done.4.got_ref = bf16[2,32,1024]{2,1,0:T(8,128)(2,1)S(1)} collective-permute-done((bf16[2,32,1024]{2,1,0:T(8,128)(2,1)S(1)}, bf16[2,32,1024]{2,1,0:T(8,128)(2,1)S(1)}, u32[]{:S(2)}, u32[]{:S(2)}) %collective-permute-start.4) | collective-permute-done | bytes 131104 | tf_op jit(solution)/shard_map/ppermute | solution.py:170
  36.6 2.0 %collective-permute-start.5 = (bf16[1,32,1024]{2,1,0:T(8,128)(2,1)S(1)}, bf16[1,32,1024]{2,1,0:T(8,128)(2,1)S(1)}, u32[]{:S(2)}, u32[]{:S(2)}) collective-permute-start(bf16[1,32,1024]{2,1,0:T(8,128)(2,1)S(1)} %get-tuple-element.17), channel_id=1, source_target_pairs={{0,24},{8,48},{16,40},{24,0},{32,56},{40,16},{48,8},{56,32},{1,25}... | collective-permute-start | bytes 196616 | tf_op jit(solution)/shard_map/ppermute | solution.py:170
  38.6 0.0 all-to-all-done.l_ref
  38.6 0.8 %shard_map.79 = bf16[8,32,1024]{2,1,0:T(8,128)(2,1)} custom-call(bf16[8,32,1024]{2,1,0:T(8,128)(2,1)S(1)} %all-to-all-done.l_ref), custom_call_target="tpu_custom_call" | custom-call | bytes 1048576 | tf_op jit(solution)/shard_map/pallas_call | solution.py:223
  39.4 3.5 %collective-permute-done.5.got_ref = bf16[1,32,1024]{2,1,0:T(8,128)(2,1)S(1)} collective-permute-done((bf16[1,32,1024]{2,1,0:T(8,128)(2,1)S(1)}, bf16[1,32,1024]{2,1,0:T(8,128)(2,1)S(1)}, u32[]{:S(2)}, u32[]{:S(2)}) %collective-permute-start.5) | collective-permute-done | bytes 65568 | tf_op jit(solution)/shard_map/ppermute | solution.py:170
  42.9 0.8 %shard_map.84 = f32[32,1,1024]{2,1,0:T(1,128)} custom-call(f32[1,32,1024]{2,1,0:T(8,128)S(1)} %get-tuple-element.16.kept_ref, bf16[1,32,1024]{2,1,0:T(8,128)(2,1)S(1)} %collective-permute-done.5.got_ref), custom_call_target="tpu_custom_call" | custom-call | bytes 1048576 | tf_op jit(solution)/shard_map/pallas_call | solution.py:224
  (2 shorter events, 0.1 us)
Async XLA Ops:
  7.4 6.8 %collective-permute-start = (bf16[72,1024]{1,0:T(8,128)(2,1)S(1)}, bf16[72,1024]{1,0:T(8,128)(2,1)S(1)}, u32[]{:S(2)}, u32[]{:S(2)}) collective-permute-start(bf16[72,1024]{1,0:T(8,128)(2,1)S(1)} %shard_map.77.fac_ref.f0_ref), channel_id=1, source_target_pairs={{0,64},{64,128},{128,192},{192,0},{1,65},{65,129},{129,193},{193,1... | collective-permute-start | bytes 442376 | tf_op jit(solution)/shard_map/ppermute | solution.py:165
  9.7 8.7 %collective-permute-start.1 = (bf16[72,1024]{1,0:T(8,128)(2,1)S(1)}, bf16[72,1024]{1,0:T(8,128)(2,1)S(1)}, u32[]{:S(2)}, u32[]{:S(2)}) collective-permute-start(bf16[72,1024]{1,0:T(8,128)(2,1)S(1)} %shard_map.77.fac_ref.f0_ref), channel_id=1, source_target_pairs={{0,192},{64,0},{128,64},{192,128},{1,193},{65,1},{129,65},{193,129... | collective-permute-start | bytes 442376 | tf_op jit(solution)/shard_map/ppermute | solution.py:165
  9.7 10.7 %collective-permute-start.2 = (bf16[72,1024]{1,0:T(8,128)(2,1)S(1)}, bf16[72,1024]{1,0:T(8,128)(2,1)S(1)}, u32[]{:S(2)}, u32[]{:S(2)}) collective-permute-start(bf16[72,1024]{1,0:T(8,128)(2,1)S(1)} %shard_map.77.fac_ref.f0_ref), channel_id=1, source_target_pairs={{0,128},{64,192},{128,0},{192,64},{1,129},{65,193},{129,1},{193,65... | collective-permute-start | bytes 442376 | tf_op jit(solution)/shard_map/ppermute | solution.py:165
  21.6 6.5 %collective-permute-start.3 = (bf16[4,32,1024]{2,1,0:T(8,128)(2,1)S(1)}, bf16[4,32,1024]{2,1,0:T(8,128)(2,1)S(1)}, u32[]{:S(2)}, u32[]{:S(2)}) collective-permute-start(bf16[4,32,1024]{2,1,0:T(8,128)(2,1)S(1)} %get-tuple-element.13), channel_id=1, source_target_pairs={{0,8},{8,0},{16,24},{24,16},{32,40},{40,32},{48,56},{56,48},{1,9},... | collective-permute-start | bytes 786440 | tf_op jit(solution)/shard_map/ppermute | solution.py:170
  22.8 15.8 %all-to-all-start = ((bf16[8,32,1024]{2,1,0:T(8,128)(2,1)}), bf16[8,32,1024]{2,1,0:T(8,128)(2,1)S(1)}, u32[]{:S(2)}, u32[]{:S(2)}) async-start(bf16[8,32,1024]{2,1,0:T(8,128)(2,1)} %bitcast.5), calls=%async_computation | async-start | bytes 1048576 | tf_op jit(solution)/shard_map/all_to_all | solution.py:209
  28.1 8.5 %collective-permute-start.4 = (bf16[2,32,1024]{2,1,0:T(8,128)(2,1)S(1)}, bf16[2,32,1024]{2,1,0:T(8,128)(2,1)S(1)}, u32[]{:S(2)}, u32[]{:S(2)}) collective-permute-start(bf16[2,32,1024]{2,1,0:T(8,128)(2,1)S(1)} %get-tuple-element.15), channel_id=1, source_target_pairs={{0,56},{8,16},{16,8},{24,32},{32,24},{40,48},{48,40},{56,0},{1,57}... | collective-permute-start | bytes 393224 | tf_op jit(solution)/shard_map/ppermute | solution.py:170
  36.6 6.3 %collective-permute-start.5 = (bf16[1,32,1024]{2,1,0:T(8,128)(2,1)S(1)}, bf16[1,32,1024]{2,1,0:T(8,128)(2,1)S(1)}, u32[]{:S(2)}, u32[]{:S(2)}) collective-permute-start(bf16[1,32,1024]{2,1,0:T(8,128)(2,1)S(1)} %get-tuple-element.17), channel_id=1, source_target_pairs={{0,24},{8,48},{16,40},{24,0},{32,56},{40,16},{48,8},{56,32},{1,25}... | collective-permute-start | bytes 196616 | tf_op jit(solution)/shard_map/ppermute | solution.py:170

commit v4 on v3

--- a/solution.py
+++ b/solution.py
@@ -83,12 +83,9 @@
     p_ref[...] = panel_of(l_ref, lax.axis_index("x"))
 
 
-def mid_part(fa_ref, fb_ref, p0_ref, p_ref, l_ref):
-    x = lax.axis_index("x")
-    seq_grads(fa_ref, l_ref)
-    acc = p0_ref[...] + panel_of(l_ref, x)
-    seq_grads(fb_ref, l_ref)
-    p_ref[...] = acc + panel_of(l_ref, x)
+def mid_part(fac_ref, p0_ref, p_ref, l_ref):
+    seq_grads(fac_ref, l_ref)
+    p_ref[...] = p0_ref[...] + panel_of(l_ref, lax.axis_index("x"))
 
 
 def hop(z, d):
@@ -207,7 +204,8 @@
     grads, part = call(own_part, [((SEQ_DEV, SQ), bf16), ((PANEL, SQ), f32)], nin=1, flops=1 << 30)(fac)
     experts = lax.axis_size("expert")
     logged = lax.all_to_all(grads.reshape(experts, SEQ_DEV // experts, SQ), "expert", 0, 0, tiled=False)
-    (part,) = call(mid_part, [((PANEL, SQ), f32)], [lbuf], nin=3, flops=2 << 30)(right, left, part)
+    for other in (right, left):
+        (part,) = call(mid_part, [((PANEL, SQ), f32)], [lbuf], nin=2, flops=1 << 30)(other, part)
     sent, kept = call(
         last_part,
         [((4, PIECE, SQ), bf16), ((4, PIECE, SQ), f32)],

time: 43.9 us -> 43.6 us (level)
  the two profiles are of different devices: /device:TPU:6 before, /device:TPU:2 now
where the time goes in v4:
time: 43.6 us; the launch traced here: 42.8 us
  starting transfers between devices  18.7 us (43%)
  Pallas kernels  12.7 us (29%)
  waiting for transfers between devices  10.1 us (23%)
  between operations  1.32 us (3%)
    ppermute x3, starting transfers between devices, swap(): return lax.ppermute(value, 'z', pairs)  9.85 us
    ppermute x3, waiting for transfers between devices, swap(): return lax.ppermute(value, 'z', pairs)  7.54 us
    pallas_call x1, Pallas kernels, step(): call(project, [((FAC, CAP), bf16)], [pltpu.VMEM((K, width), bf16), pltpu....  6.13 us
    all_to_all x1, starting transfers between devices, step(): lax.all_to_all(grads.reshape(experts, SEQ_DEV // experts, SQ), 'expert',...  4.46 us
    ppermute x3, starting transfers between devices, shift(): return lax.ppermute(value, 'x', [(i, (i + d) % NX) for i in range(NX)])  4.39 us
    ppermute x3, waiting for transfers between devices, shift(): return lax.ppermute(value, 'x', [(i, (i + d) % NX) for i in range(NX)])  2.53 us
    pallas_call x2, Pallas kernels, step(): call(mid_part, [((PANEL, SQ), f32)], [lbuf], nin=2, flops=1 << 30)  2.16 us
    pallas_call x1, Pallas kernels, step(): call(own_part, [((SEQ_DEV, SQ), bf16), ((PANEL, SQ), f32)], nin=1, flops=...  1.58 us
  transfers between devices with their start and end apart: 7, of which 5 were waited for; matrix products, arithmetic and copies ran while one was open for 0% of the time, Pallas kernels for 11%

profile of v4, /device:TPU:2, one launch (start us, length us, event | category | flops | bytes accessed | tf_op | source)
XLA Modules:
  0.0 42.8 jit_solution(14492586825735746634)
XLA Ops:
  1.3 6.1 %shard_map.77.fac_ref.f0_ref = bf16[72,1024]{1,0:T(8,128)(2,1)S(1)} custom-call(s32[1,1]{1,0:T(1,128)S(6)} %copy.8.cnt_ref, bf16[1024,4096]{1,0:T(8,128)(2,1)} %bitcast.6, bf16[1024,1536]{1,0:T(8,128)(2,1)} %bitcast.7, bf16[32,4096]{1,0:T(8,128)(2,1)} %bitcast.8, bf16[32,1536]{1,0:T(8,128)(2,1)} %bitcast.9, s32[1,1024]{1,0:T(1,128)} %bitcast.10), custom_call_target="tpu_custom_call" | custom-call | bytes 1048576 | tf_op jit(solution)/shard_map/pallas_call | solution.py:173
  7.4 1.6 %collective-permute-start = (bf16[72,1024]{1,0:T(8,128)(2,1)S(1)}, bf16[72,1024]{1,0:T(8,128)(2,1)S(1)}, u32[]{:S(2)}, u32[]{:S(2)}) collective-permute-start(bf16[72,1024]{1,0:T(8,128)(2,1)S(1)} %shard_map.77.fac_ref.f0_ref), channel_id=1, source_target_pairs={{0,64},{64,128},{128,192},{192,0},{1,65},{65,129},{129,193},{193,1... | collective-permute-start | bytes 442376 | tf_op jit(solution)/shard_map/ppermute | solution.py:162
  9.0 0.8 %collective-permute-start.1 = (bf16[72,1024]{1,0:T(8,128)(2,1)S(1)}, bf16[72,1024]{1,0:T(8,128)(2,1)S(1)}, u32[]{:S(2)}, u32[]{:S(2)}) collective-permute-start(bf16[72,1024]{1,0:T(8,128)(2,1)S(1)} %shard_map.77.fac_ref.f0_ref), channel_id=1, source_target_pairs={{0,192},{64,0},{128,64},{192,128},{1,193},{65,1},{129,65},{193,129... | collective-permute-start | bytes 442376 | tf_op jit(solution)/shard_map/ppermute | solution.py:162
  9.8 2.0 %collective-permute-start.2 = (bf16[72,1024]{1,0:T(8,128)(2,1)S(1)}, bf16[72,1024]{1,0:T(8,128)(2,1)S(1)}, u32[]{:S(2)}, u32[]{:S(2)}) collective-permute-start(bf16[72,1024]{1,0:T(8,128)(2,1)S(1)} %shard_map.77.fac_ref.f0_ref), channel_id=1, source_target_pairs={{0,128},{64,192},{128,0},{192,64},{1,129},{65,193},{129,1},{193,65... | collective-permute-start | bytes 442376 | tf_op jit(solution)/shard_map/ppermute | solution.py:162
  11.8 1.6 %shard_map.78 = (bf16[256,1024]{1,0:T(8,128)(2,1)}, f32[256,1024]{1,0:T(8,128)S(1)}) custom-call(bf16[72,1024]{1,0:T(8,128)(2,1)S(1)} %shard_map.77.fac_ref.f0_ref), custom_call_target="tpu_custom_call" | custom-call | flops 1073741824 | bytes 1048576 | tf_op jit(solution)/shard_map/pallas_call | solution.py:204
  13.4 0.0 collective-permute-done.fac_ref.fa_ref
  13.4 1.1 %shard_map.80.p0_ref = f32[256,1024]{1,0:T(8,128)S(1)} custom-call(bf16[72,1024]{1,0:T(8,128)(2,1)S(1)} %collective-permute-done.fac_ref.fa_ref, f32[256,1024]{1,0:T(8,128)S(1)} %get-tuple-element.11.p0_ref), custom_call_target="tpu_custom_call" | custom-call | flops 1073741824 | bytes 1048576 | tf_op jit(solution)/shard_map/pallas_call | solution.py:208
  14.5 0.8 %collective-permute-done.1.fac_ref.fb_ref = bf16[72,1024]{1,0:T(8,128)(2,1)S(1)} collective-permute-done((bf16[72,1024]{1,0:T(8,128)(2,1)S(1)}, bf16[72,1024]{1,0:T(8,128)(2,1)S(1)}, u32[]{:S(2)}, u32[]{:S(2)}) %collective-permute-start.1) | collective-permute-done | bytes 147488 | tf_op jit(solution)/shard_map/ppermute | solution.py:162
  15.2 1.1 %shard_map.81.p1_ref = f32[256,1024]{1,0:T(8,128)S(1)} custom-call(bf16[72,1024]{1,0:T(8,128)(2,1)S(1)} %collective-permute-done.1.fac_ref.fb_ref, f32[256,1024]{1,0:T(8,128)S(1)} %shard_map.80.p0_ref), custom_call_target="tpu_custom_call" | custom-call | flops 1073741824 | bytes 1048576 | tf_op jit(solution)/shard_map/pallas_call | solution.py:208
  16.3 1.8 %collective-permute-done.2.fc_ref = bf16[72,1024]{1,0:T(8,128)(2,1)S(1)} collective-permute-done((bf16[72,1024]{1,0:T(8,128)(2,1)S(1)}, bf16[72,1024]{1,0:T(8,128)(2,1)S(1)}, u32[]{:S(2)}, u32[]{:S(2)}) %collective-permute-start.2) | collective-permute-done | bytes 147488 | tf_op jit(solution)/shard_map/ppermute | solution.py:162
  18.1 1.2 %shard_map.82 = (bf16[4,32,1024]{2,1,0:T(8,128)(2,1)S(1)}, f32[4,32,1024]{2,1,0:T(8,128)S(1)}) custom-call(bf16[72,1024]{1,0:T(8,128)(2,1)S(1)} %shard_map.77.fac_ref.f0_ref, bf16[72,1024]{1,0:T(8,128)(2,1)S(1)} %collective-permute-done.fac_ref.fa_ref, bf16[72,1024]{1,0:T(8,128)(2,1)S(1)} %collective-permute-done.1.fac_ref.fb_ref, ...), custom_call_target="tpu_custom_call" | custom-call | flops 1073741824 | bytes 1048576 | tf_op jit(solution)/shard_map/pallas_call | solution.py:209
  19.3 2.0 %collective-permute-start.3 = (bf16[4,32,1024]{2,1,0:T(8,128)(2,1)S(1)}, bf16[4,32,1024]{2,1,0:T(8,128)(2,1)S(1)}, u32[]{:S(2)}, u32[]{:S(2)}) collective-permute-start(bf16[4,32,1024]{2,1,0:T(8,128)(2,1)S(1)} %get-tuple-element.13), channel_id=1, source_target_pairs={{0,8},{8,0},{16,24},{24,16},{32,40},{40,32},{48,56},{56,48},{1,9},... | collective-permute-start | bytes 786440 | tf_op jit(solution)/shard_map/ppermute | solution.py:167
  21.3 4.5 %all-to-all-start = ((bf16[8,32,1024]{2,1,0:T(8,128)(2,1)}), bf16[8,32,1024]{2,1,0:T(8,128)(2,1)S(1)}, u32[]{:S(2)}, u32[]{:S(2)}) async-start(bf16[8,32,1024]{2,1,0:T(8,128)(2,1)} %bitcast.5), calls=%async_computation | async-start | bytes 1048576 | tf_op jit(solution)/shard_map/all_to_all | solution.py:206
  25.7 0.7 %collective-permute-done.3.got_ref = bf16[4,32,1024]{2,1,0:T(8,128)(2,1)S(1)} collective-permute-done((bf16[4,32,1024]{2,1,0:T(8,128)(2,1)S(1)}, bf16[4,32,1024]{2,1,0:T(8,128)(2,1)S(1)}, u32[]{:S(2)}, u32[]{:S(2)}) %collective-permute-start.3) | collective-permute-done | bytes 262176 | tf_op jit(solution)/shard_map/ppermute | solution.py:167
  26.5 5.8 %collective-permute-start.4 = (bf16[2,32,1024]{2,1,0:T(8,128)(2,1)S(1)}, bf16[2,32,1024]{2,1,0:T(8,128)(2,1)S(1)}, u32[]{:S(2)}, u32[]{:S(2)}) collective-permute-start(bf16[2,32,1024]{2,1,0:T(8,128)(2,1)S(1)} %get-tuple-element.15), channel_id=1, source_target_pairs={{0,56},{8,16},{16,8},{24,32},{32,24},{40,48},{48,40},{56,0},{1,57}... | collective-permute-start | bytes 393224 | tf_op jit(solution)/shard_map/ppermute | solution.py:167
  32.2 2.9 %collective-permute-done.4.got_ref = bf16[2,32,1024]{2,1,0:T(8,128)(2,1)S(1)} collective-permute-done((bf16[2,32,1024]{2,1,0:T(8,128)(2,1)S(1)}, bf16[2,32,1024]{2,1,0:T(8,128)(2,1)S(1)}, u32[]{:S(2)}, u32[]{:S(2)}) %collective-permute-start.4) | collective-permute-done | bytes 131104 | tf_op jit(solution)/shard_map/ppermute | solution.py:167
  35.2 2.1 %collective-permute-start.5 = (bf16[1,32,1024]{2,1,0:T(8,128)(2,1)S(1)}, bf16[1,32,1024]{2,1,0:T(8,128)(2,1)S(1)}, u32[]{:S(2)}, u32[]{:S(2)}) collective-permute-start(bf16[1,32,1024]{2,1,0:T(8,128)(2,1)S(1)} %get-tuple-element.17), channel_id=1, source_target_pairs={{0,24},{8,48},{16,40},{24,0},{32,56},{40,16},{48,8},{56,32},{1,25}... | collective-permute-start | bytes 196616 | tf_op jit(solution)/shard_map/ppermute | solution.py:167
  37.3 0.0 all-to-all-done.l_ref
  37.3 0.8 %shard_map.79 = bf16[8,32,1024]{2,1,0:T(8,128)(2,1)} custom-call(bf16[8,32,1024]{2,1,0:T(8,128)(2,1)S(1)} %all-to-all-done.l_ref), custom_call_target="tpu_custom_call" | custom-call | bytes 1048576 | tf_op jit(solution)/shard_map/pallas_call | solution.py:221
  38.1 3.9 %collective-permute-done.5.got_ref = bf16[1,32,1024]{2,1,0:T(8,128)(2,1)S(1)} collective-permute-done((bf16[1,32,1024]{2,1,0:T(8,128)(2,1)S(1)}, bf16[1,32,1024]{2,1,0:T(8,128)(2,1)S(1)}, u32[]{:S(2)}, u32[]{:S(2)}) %collective-permute-start.5) | collective-permute-done | bytes 65568 | tf_op jit(solution)/shard_map/ppermute | solution.py:167
  42.0 0.8 %shard_map.85 = f32[32,1,1024]{2,1,0:T(1,128)} custom-call(f32[1,32,1024]{2,1,0:T(8,128)S(1)} %get-tuple-element.16.kept_ref, bf16[1,32,1024]{2,1,0:T(8,128)(2,1)S(1)} %collective-permute-done.5.got_ref), custom_call_target="tpu_custom_call" | custom-call | bytes 1048576 | tf_op jit(solution)/shard_map/pallas_call | solution.py:222
  (2 shorter events, 0.1 us)
Async XLA Ops:
  7.4 6.0 %collective-permute-start = (bf16[72,1024]{1,0:T(8,128)(2,1)S(1)}, bf16[72,1024]{1,0:T(8,128)(2,1)S(1)}, u32[]{:S(2)}, u32[]{:S(2)}) collective-permute-start(bf16[72,1024]{1,0:T(8,128)(2,1)S(1)} %shard_map.77.fac_ref.f0_ref), channel_id=1, source_target_pairs={{0,64},{64,128},{128,192},{192,0},{1,65},{65,129},{129,193},{193,1... | collective-permute-start | bytes 442376 | tf_op jit(solution)/shard_map/ppermute | solution.py:162
  9.0 6.2 %collective-permute-start.1 = (bf16[72,1024]{1,0:T(8,128)(2,1)S(1)}, bf16[72,1024]{1,0:T(8,128)(2,1)S(1)}, u32[]{:S(2)}, u32[]{:S(2)}) collective-permute-start(bf16[72,1024]{1,0:T(8,128)(2,1)S(1)} %shard_map.77.fac_ref.f0_ref), channel_id=1, source_target_pairs={{0,192},{64,0},{128,64},{192,128},{1,193},{65,1},{129,65},{193,129... | collective-permute-start | bytes 442376 | tf_op jit(solution)/shard_map/ppermute | solution.py:162
  9.8 8.3 %collective-permute-start.2 = (bf16[72,1024]{1,0:T(8,128)(2,1)S(1)}, bf16[72,1024]{1,0:T(8,128)(2,1)S(1)}, u32[]{:S(2)}, u32[]{:S(2)}) collective-permute-start(bf16[72,1024]{1,0:T(8,128)(2,1)S(1)} %shard_map.77.fac_ref.f0_ref), channel_id=1, source_target_pairs={{0,128},{64,192},{128,0},{192,64},{1,129},{65,193},{129,1},{193,65... | collective-permute-start | bytes 442376 | tf_op jit(solution)/shard_map/ppermute | solution.py:162
  19.3 7.2 %collective-permute-start.3 = (bf16[4,32,1024]{2,1,0:T(8,128)(2,1)S(1)}, bf16[4,32,1024]{2,1,0:T(8,128)(2,1)S(1)}, u32[]{:S(2)}, u32[]{:S(2)}) collective-permute-start(bf16[4,32,1024]{2,1,0:T(8,128)(2,1)S(1)} %get-tuple-element.13), channel_id=1, source_target_pairs={{0,8},{8,0},{16,24},{24,16},{32,40},{40,32},{48,56},{56,48},{1,9},... | collective-permute-start | bytes 786440 | tf_op jit(solution)/shard_map/ppermute | solution.py:167
  21.3 16.0 %all-to-all-start = ((bf16[8,32,1024]{2,1,0:T(8,128)(2,1)}), bf16[8,32,1024]{2,1,0:T(8,128)(2,1)S(1)}, u32[]{:S(2)}, u32[]{:S(2)}) async-start(bf16[8,32,1024]{2,1,0:T(8,128)(2,1)} %bitcast.5), calls=%async_computation | async-start | bytes 1048576 | tf_op jit(solution)/shard_map/all_to_all | solution.py:206
  26.5 8.7 %collective-permute-start.4 = (bf16[2,32,1024]{2,1,0:T(8,128)(2,1)S(1)}, bf16[2,32,1024]{2,1,0:T(8,128)(2,1)S(1)}, u32[]{:S(2)}, u32[]{:S(2)}) collective-permute-start(bf16[2,32,1024]{2,1,0:T(8,128)(2,1)S(1)} %get-tuple-element.15), channel_id=1, source_target_pairs={{0,56},{8,16},{16,8},{24,32},{32,24},{40,48},{48,40},{56,0},{1,57}... | collective-permute-start | bytes 393224 | tf_op jit(solution)/shard_map/ppermute | solution.py:167
  35.2 6.8 %collective-permute-start.5 = (bf16[1,32,1024]{2,1,0:T(8,128)(2,1)S(1)}, bf16[1,32,1024]{2,1,0:T(8,128)(2,1)S(1)}, u32[]{:S(2)}, u32[]{:S(2)}) collective-permute-start(bf16[1,32,1024]{2,1,0:T(8,128)(2,1)S(1)} %get-tuple-element.17), channel_id=1, source_target_pairs={{0,24},{8,48},{16,40},{24,0},{32,56},{40,16},{48,8},{56,32},{1,25}... | collective-permute-start | bytes 196616 | tf_op jit(solution)/shard_map/ppermute | solution.py:167
